TPU v7x, 256 devices: a whole 4x4x8 slice. The times are simulated.
256 devices in a mesh: dp: 8 (over x, core), expert: 32 (over z, y).
Axes of the slice: x: 4, y: 4, z: 8, core: 2. Of those that a mesh axis runs over, the one named last changes fastest.
Arguments:
- tokens: bfloat16 [12288, 2048], P(('dp', 'expert')), may hold values from -6 to 6
- expert_ids: int32 [12288, 8], P(('dp', 'expert')), may hold values from 0 to 31, all different within a row; in each aligned block of 48 rows (0 to 47, 48 to 95, ...) at most 16 rows name the same one
- gate_probs: float32 [12288, 8], P(('dp', 'expert')), may hold values from 0.05 to 0.5
- out_cot: bfloat16 [12288, 2048], P(('dp', 'expert')), may hold values from -1.5 to 1.5
- w_gate: bfloat16 [32, 2048, 768], P('expert'), may hold values from -0.125 to 0.125
- w_up: bfloat16 [32, 2048, 768], P('expert'), may hold values from -0.125 to 0.125
- w_down: bfloat16 [32, 768, 2048], P('expert'), may hold values from -0.21875 to 0.21875
Outputs:
- layer_out: bfloat16 [12288, 2048], P(('dp', 'expert'))
- input_grad: bfloat16 [12288, 2048], P(('dp', 'expert'))
- gate_wgrad: float32 [32, 2048, 768], P('expert', 'dp')
- up_wgrad: float32 [32, 2048, 768], P('expert', 'dp')
- down_wgrad: float32 [32, 768, 2048], P('expert', 'dp')
Inputs may be any that keep to these rules, and one draw needn't show every extreme that they name: `expert_ids`: each token names 8 different experts. Among the 48 tokens of one device, at most 16 name the same expert, and in every draw some expert is named by exactly 16 tokens of some device.
All inputs are finite; a program needn't handle non-finite values.
Results may differ from a plain program's by a relative error of at most 0.012.
Values may be sent and summed in bfloat16 or wider, within the bound.
A program may use at most 128 MiB of HBM per device.

v0:
```python
import jax
import jax.numpy as jnp
from jax import lax
from jax.sharding import PartitionSpec as P


def contract_rows(left, right):
    return lax.dot_general(
        left, right, (((0,), (0,)), ((), ())), preferred_element_type=jnp.float32
    )


def contract_cols(left, right):
    return lax.dot_general(
        left, right, (((1,), (1,)), ((), ())), preferred_element_type=jnp.float32
    )


def shards(tokens, expert_ids, gate_probs, out_cot, w_gate, w_up, w_down):
    tok_count, width = tokens.shape
    top = expert_ids.shape[1]
    experts = lax.axis_size("expert")
    slots = min(tok_count, 4 * tok_count * top // (3 * experts))
    flat_ids = expert_ids.reshape(-1)
    onehot = (flat_ids[:, None] == jnp.arange(experts, dtype=jnp.int32)[None, :]).astype(jnp.int32)
    ranks = jnp.sum(jnp.cumsum(onehot, axis=0) * onehot, axis=1) - 1
    target = flat_ids * slots + ranks
    token_rows = jnp.repeat(tokens, top, axis=0)
    outbound = jnp.zeros((experts * slots, width), tokens.dtype).at[target].set(token_rows)
    outbound = outbound.reshape(experts, slots, width)
    gate_mat = w_gate[0]
    up_mat = w_up[0]
    down_mat = w_down[0]
    hidden_width = gate_mat.shape[1]
    arrived = lax.all_to_all(outbound, "expert", split_axis=0, concat_axis=0, tiled=True)
    sources = arrived.shape[0]
    count = arrived.shape[1]
    rows = arrived.reshape(-1, width)
    gate_pre = jnp.dot(rows, gate_mat, preferred_element_type=jnp.float32)
    up_pre = jnp.dot(rows, up_mat, preferred_element_type=jnp.float32)
    hidden = (gate_pre * jax.nn.sigmoid(gate_pre) * up_pre).astype(jnp.bfloat16)
    result = jnp.dot(hidden, down_mat, preferred_element_type=jnp.float32).astype(jnp.bfloat16)
    expert_out, hidden, gate_pre, up_pre, arrived = (
        result.reshape(sources, count, width),
        hidden.reshape(sources, count, hidden_width),
        gate_pre.reshape(sources, count, hidden_width),
        up_pre.reshape(sources, count, hidden_width),
        arrived,
    )
    returned = lax.all_to_all(expert_out, "expert", split_axis=0, concat_axis=0, tiled=True)
    picked = returned.reshape(-1, width)[target].reshape(tok_count, top, width)
    layer_out = jnp.sum(gate_probs[:, :, None] * picked.astype(jnp.float32), axis=1).astype(
        jnp.bfloat16
    )
    out_grad = (gate_probs[:, :, None] * out_cot[:, None, :].astype(jnp.float32)).astype(
        jnp.bfloat16
    )
    outbound_grad = (
        jnp.zeros((experts * slots, width), tokens.dtype)
        .at[target]
        .set(out_grad.reshape(-1, width))
    )
    arrived_grad = lax.all_to_all(
        outbound_grad.reshape(experts, slots, width),
        "expert",
        split_axis=0,
        concat_axis=0,
        tiled=True,
    ).reshape(-1, width)
    x_rows = arrived.reshape(-1, width)
    hidden_rows = hidden.reshape(-1, hidden_width)
    gate_rows = gate_pre.reshape(-1, hidden_width)
    up_rows = up_pre.reshape(-1, hidden_width)
    hidden_grad = contract_cols(arrived_grad, down_mat)
    sigma = jax.nn.sigmoid(gate_rows)
    gate_grad = (hidden_grad * up_rows * sigma * (1.0 + gate_rows * (1.0 - sigma))).astype(
        jnp.bfloat16
    )
    up_grad = (hidden_grad * gate_rows * sigma).astype(jnp.bfloat16)
    row_grad = (contract_cols(gate_grad, gate_mat) + contract_cols(up_grad, up_mat)).astype(
        jnp.bfloat16
    )
    back_grad = lax.all_to_all(
        row_grad.reshape(experts, slots, width), "expert", split_axis=0, concat_axis=0, tiled=True
    )
    gathered = back_grad.reshape(-1, width)[target].reshape(tok_count, top, width)
    input_grad = jnp.sum(gathered.astype(jnp.float32), axis=1).astype(jnp.bfloat16)
    down_grad = lax.psum_scatter(
        contract_rows(hidden_rows, arrived_grad).astype(jnp.bfloat16),
        "dp",
        scatter_dimension=0,
        tiled=True,
    ).astype(jnp.float32)
    gate_part = lax.psum_scatter(
        contract_rows(x_rows, gate_grad).astype(jnp.bfloat16), "dp", scatter_dimension=0, tiled=True
    ).astype(jnp.float32)
    up_part = lax.psum_scatter(
        contract_rows(x_rows, up_grad).astype(jnp.bfloat16), "dp", scatter_dimension=0, tiled=True
    ).astype(jnp.float32)
    return (layer_out, input_grad, gate_part[None], up_part[None], down_grad[None])


def solution(mesh):
    placed = (
        P(("dp", "expert"), None),
        P(("dp", "expert"), None),
        P(("dp", "expert"), None),
        P(("dp", "expert"), None),
        P("expert", None, None),
        P("expert", None, None),
        P("expert", None, None),
    )
    return jax.shard_map(
        shards,
        mesh=mesh,
        in_specs=placed,
        out_specs=(
            P(("dp", "expert"), None),
            P(("dp", "expert"), None),
            P("expert", "dp", None),
            P("expert", "dp", None),
            P("expert", "dp", None),
        ),
        check_vma=False,
    )
```

profile of v0, /device:TPU:8, one launch (start us, length us, event | category | flops | bytes accessed | tf_op | source)
XLA Modules:
  0.0 293.4 jit_solution(9378216640644673959)
XLA Ops:
  12.9 4.4 %scatter_custom_fusion.1 = bf16[512,2048]{1,0:T(8,128)(2,1)} fusion(s32[384]{0:T(512)S(1)} %fusion.31, f32[48,2048]{1,0:T(8,128)S(1)} %convert_element_type.57, f32[384]{0:T(512)S(1)} %mul.77, bf16[]{:T(256)} %constant.7.clone.1), kind=kCustom, calls=%fused_computation.25 | custom fusion | flops 1572864 | bytes 2492418 | tf_op jit(solution)/shard_map/scatter | solution.py:61
  17.3 11.9 %all-to-all-start.2 = ((bf16[32,16,2048]{2,1,0:T(8,128)(2,1)}), bf16[32,16,2048]{2,1,0:T(8,128)(2,1)}, u32[]{:S(2)}, u32[]{:S(2)}) async-start(bf16[32,16,2048]{2,1,0:T(8,128)(2,1)} %bitcast.82), calls=%async_computation.2 | async-start | bytes 4194304 | tf_op jit(solution)/shard_map/all_to_all | solution.py:63
  29.2 4.4 %scatter_custom_fusion = bf16[512,2048]{1,0:T(8,128)(2,1)} fusion(s32[384]{0:T(512)S(1)} %fusion.31, bf16[]{:T(256)} %constant.7.clone.1, bf16[48,2048]{1,0:T(8,128)(2,1)S(1)} %copy-done.4), kind=kCustom, calls=%fused_computation.27 | custom fusion | bytes 2293762 | tf_op jit(solution)/shard_map/scatter | solution.py:29
  33.7 44.8 %all-to-all-done.2 = bf16[32,16,2048]{2,1,0:T(8,128)(2,1)} async-done(((bf16[32,16,2048]{2,1,0:T(8,128)(2,1)}), bf16[32,16,2048]{2,1,0:T(8,128)(2,1)}, u32[]{:S(2)}, u32[]{:S(2)}) %all-to-all-start.2) | async-done | bytes 2097184 | tf_op jit(solution)/shard_map/all_to_all | solution.py:63
  78.5 6.9 %all-to-all-start = ((bf16[32,16,2048]{2,1,0:T(8,128)(2,1)}), bf16[32,16,2048]{2,1,0:T(8,128)(2,1)}, u32[]{:S(2)}, u32[]{:S(2)}) async-start(bf16[32,16,2048]{2,1,0:T(8,128)(2,1)} %bitcast.81), calls=%async_computation | async-start | bytes 4194304 | tf_op jit(solution)/shard_map/all_to_all | solution.py:35
  85.7 5.5 %fusion.2 = f32[512,768]{1,0:T(8,128)} fusion(bf16[512,2048]{1,0:T(8,128)(2,1)} %bitcast.12, bf16[1,768,2048]{2,1,0:T(8,128)(2,1)} %param.13), kind=kOutput, calls=%fused_computation.12 | convolution fusion | flops 1610612736 | bytes 6815744 | tf_op jit(solution)/shard_map/dot_general | solution.py:14
  91.2 42.9 %all-to-all-done = bf16[32,16,2048]{2,1,0:T(8,128)(2,1)} async-done(((bf16[32,16,2048]{2,1,0:T(8,128)(2,1)}), bf16[32,16,2048]{2,1,0:T(8,128)(2,1)}, u32[]{:S(2)}, u32[]{:S(2)}) %all-to-all-start) | async-done | bytes 2097184 | tf_op jit(solution)/shard_map/all_to_all | solution.py:35
  134.0 4.4 %fusion.8 = f32[512,768]{1,0:T(8,128)S(1)} fusion(bf16[512,2048]{1,0:T(8,128)(2,1)} %bitcast.3, bf16[1,2048,768]{2,1,0:T(8,128)(2,1)} %param.12), kind=kOutput, calls=%fused_computation.18 | convolution fusion | flops 1610612736 | bytes 6815744 | tf_op jit(solution)/shard_map/dot_general | solution.py:40
  138.5 5.1 %multiply_convert_fusion.1 = (bf16[512,768]{1,0:T(8,128)(2,1)S(1)}, bf16[512,768]{1,0:T(8,128)(2,1)}, bf16[512,768]{1,0:T(8,128)(2,1)}) fusion(f32[512,768]{1,0:T(8,128)S(1)} %copy-done.7, f32[512,768]{1,0:T(8,128)S(1)} %fusion.8, bf16[512,2048]{1,0:T(8,128)(2,1)} %bitcast.3, bf16[1,2048,768]{2,1,0:T(8,128)(2,1)S(1)} %copy-done), kind=kOutput, calls=%fused_computation.30 | convolution fusion | flops 1616904192 | bytes 10747904 | tf_op jit(solution)/shard_map/dot_general | solution.py:39
  144.4 5.1 %convolution_convert_fusion.2 = bf16[2048,768]{1,0:T(8,128)(2,1)} fusion(bf16[512,2048]{1,0:T(8,128)(2,1)} %bitcast.3, bf16[512,768]{1,0:T(8,128)(2,1)S(1)} %get-tuple-element.5), kind=kOutput, calls=%fused_computation.7 | convolution fusion | flops 1612185600 | bytes 6029312 | tf_op jit(solution)/shard_map/dot_general | solution.py:8
  149.6 5.4 %convolution_convert_fusion = bf16[768,2048]{1,0:T(8,128)(2,1)} fusion(bf16[512,768]{1,0:T(8,128)(2,1)} %get-tuple-element.6, bf16[512,2048]{1,0:T(8,128)(2,1)} %bitcast.12), kind=kOutput, calls=%fused_computation.5 | convolution fusion | flops 1612185600 | bytes 6029312 | tf_op jit(solution)/shard_map/dot_general | solution.py:8
  155.0 5.3 %fusion.14 = bf16[512,2048]{1,0:T(8,128)(2,1)} fusion(bf16[512,768]{1,0:T(8,128)(2,1)} %get-tuple-element.6, bf16[1,768,2048]{2,1,0:T(8,128)(2,1)} %param.13), kind=kOutput, calls=%fused_computation.24 | convolution fusion | flops 1611661312 | bytes 6029312 | tf_op jit(solution)/shard_map/dot_general | solution.py:42
  160.3 6.6 %all-to-all-start.1 = ((bf16[32,16,2048]{2,1,0:T(8,128)(2,1)}), bf16[32,16,2048]{2,1,0:T(8,128)(2,1)}, u32[]{:S(2)}, u32[]{:S(2)}) async-start(bf16[32,16,2048]{2,1,0:T(8,128)(2,1)} %bitcast.83), calls=%async_computation.1 | async-start | bytes 4194304 | tf_op jit(solution)/shard_map/all_to_all | solution.py:50
  167.2 5.3 %convolution_convert_fusion.1 = bf16[2048,768]{1,0:T(8,128)(2,1)} fusion(bf16[512,2048]{1,0:T(8,128)(2,1)} %bitcast.3, bf16[512,768]{1,0:T(8,128)(2,1)} %get-tuple-element.7), kind=kOutput, calls=%fused_computation.6 | convolution fusion | flops 1612185600 | bytes 6029312 | tf_op jit(solution)/shard_map/dot_general | solution.py:8
  172.5 4.1 %fusion.6 = f32[512,2048]{1,0:T(8,128)S(1)} fusion(bf16[512,768]{1,0:T(8,128)(2,1)} %get-tuple-element.7, bf16[1,2048,768]{2,1,0:T(8,128)(2,1)} %param.12), kind=kOutput, calls=%fused_computation.16 | convolution fusion | flops 1610612736 | bytes 8126464 | tf_op jit(solution)/shard_map/dot_general | solution.py:14
  176.6 3.2 %add_convert_fusion = bf16[512,2048]{1,0:T(8,128)(2,1)} fusion(f32[512,2048]{1,0:T(8,128)S(1)} %fusion.6, bf16[512,768]{1,0:T(8,128)(2,1)S(1)} %copy-done.6, bf16[1,2048,768]{2,1,0:T(8,128)(2,1)S(1)} %copy-done), kind=kOutput, calls=%fused_computation.4 | convolution fusion | flops 1612709888 | bytes 10223616 | tf_op jit(solution)/shard_map/dot_general | solution.py:14
  179.8 36.0 %all-to-all-done.1 = bf16[32,16,2048]{2,1,0:T(8,128)(2,1)} async-done(((bf16[32,16,2048]{2,1,0:T(8,128)(2,1)}), bf16[32,16,2048]{2,1,0:T(8,128)(2,1)}, u32[]{:S(2)}, u32[]{:S(2)}) %all-to-all-start.1) | async-done | bytes 2097184 | tf_op jit(solution)/shard_map/all_to_all | solution.py:50
  215.9 5.6 %all-to-all-start.3 = ((bf16[32,16,2048]{2,1,0:T(8,128)(2,1)}), bf16[32,16,2048]{2,1,0:T(8,128)(2,1)}, u32[]{:S(2)}, u32[]{:S(2)}) async-start(bf16[32,16,2048]{2,1,0:T(8,128)(2,1)} %bitcast.84), calls=%async_computation.3 | async-start | bytes 4194304 | tf_op jit(solution)/shard_map/all_to_all | solution.py:83
  221.5 6.9 %gather_fusion = bf16[384,2048]{1,0:T(8,128)(2,1)} fusion(bf16[512,2048]{1,0:T(8,128)(2,1)} %bitcast.8, s32[1024]{0:T(1024)S(1)} %pad_clamp_fusion), kind=kCustom, calls=%fused_computation | custom fusion | bytes 3147264 | tf_op jit(solution)/shard_map/gather | solution.py:51
  228.4 40.3 %all-to-all-done.3 = bf16[32,16,2048]{2,1,0:T(8,128)(2,1)} async-done(((bf16[32,16,2048]{2,1,0:T(8,128)(2,1)}), bf16[32,16,2048]{2,1,0:T(8,128)(2,1)}, u32[]{:S(2)}, u32[]{:S(2)}) %all-to-all-start.3) | async-done | bytes 2097184 | tf_op jit(solution)/shard_map/all_to_all | solution.py:83
  268.8 6.9 %gather_fusion.1 = bf16[384,2048]{1,0:T(8,128)(2,1)} fusion(bf16[512,2048]{1,0:T(8,128)(2,1)} %bitcast.14, s32[1024]{0:T(1024)S(1)} %pad_clamp_fusion), kind=kCustom, calls=%fused_computation.1 | custom fusion | bytes 3147264 | tf_op jit(solution)/shard_map/gather | solution.py:86
  275.7 3.3 %bitcast_reduce_fusion = bf16[48,2048]{1,0:T(8,128)(2,1)} fusion(bf16[384,2048]{1,0:T(8,128)(2,1)} %gather_fusion.1), kind=kLoop, calls=%fused_computation.26 | loop fusion | flops 688128 | bytes 1769472 | tf_op jit(solution)/shard_map/reduce_sum | solution.py:87
  279.0 2.1 fusion
  283.0 1.9 bitcast_convert_fusion
  (44 shorter events, 11.0 us)
Async XLA Ops:
  7.2 131.3 %copy-start = (bf16[1,2048,768]{2,1,0:T(8,128)(2,1)S(1)}, bf16[1,2048,768]{2,1,0:T(8,128)(2,1)}, u32[]{:S(2)}) copy-start(bf16[1,2048,768]{2,1,0:T(8,128)(2,1)} %param.11) | copy-start | bytes 9437188
  10.0 0.6 copy-start.2
  17.3 11.9 %copy-start.4 = (bf16[48,2048]{1,0:T(8,128)(2,1)S(1)}, bf16[48,2048]{1,0:T(8,128)(2,1)}, u32[]{:S(2)}) copy-start(bf16[48,2048]{1,0:T(8,128)(2,1)} %param.7) | copy-start | bytes 589828
  17.3 61.2 %all-to-all-start.2 = ((bf16[32,16,2048]{2,1,0:T(8,128)(2,1)}), bf16[32,16,2048]{2,1,0:T(8,128)(2,1)}, u32[]{:S(2)}, u32[]{:S(2)}) async-start(bf16[32,16,2048]{2,1,0:T(8,128)(2,1)} %bitcast.82), calls=%async_computation.2 | async-start | bytes 4194304 | tf_op jit(solution)/shard_map/all_to_all | solution.py:63
  78.5 55.5 %all-to-all-start = ((bf16[32,16,2048]{2,1,0:T(8,128)(2,1)}), bf16[32,16,2048]{2,1,0:T(8,128)(2,1)}, u32[]{:S(2)}, u32[]{:S(2)}) async-start(bf16[32,16,2048]{2,1,0:T(8,128)(2,1)} %bitcast.81), calls=%async_computation | async-start | bytes 4194304 | tf_op jit(solution)/shard_map/all_to_all | solution.py:35
  85.4 195.7 %reduce-scatter.4.cloned.1.call-start = ((), (), s32[]{:S(2)}) async-start(), calls=%async_computation.7 | async-start | bytes 3538944 | tf_op jit(solution)/shard_map/reduce_scatter | solution.py:94
  134.0 4.4 %copy-start.7 = (f32[512,768]{1,0:T(8,128)S(1)}, f32[512,768]{1,0:T(8,128)}, u32[]{:S(2)}) copy-start(f32[512,768]{1,0:T(8,128)} %fusion.2) | copy-start | bytes 4718596
  143.6 0.9 copy-start.5
  149.6 133.5 %reduce-scatter.8.cloned.1.call-start = ((), (), s32[]{:S(2)}) async-start(), calls=%async_computation.9 | async-start | bytes 3538944 | tf_op jit(solution)/shard_map/reduce_scatter | solution.py:88
  160.3 55.6 %all-to-all-start.1 = ((bf16[32,16,2048]{2,1,0:T(8,128)(2,1)}), bf16[32,16,2048]{2,1,0:T(8,128)(2,1)}, u32[]{:S(2)}, u32[]{:S(2)}) async-start(bf16[32,16,2048]{2,1,0:T(8,128)(2,1)} %bitcast.83), calls=%async_computation.1 | async-start | bytes 4194304 | tf_op jit(solution)/shard_map/all_to_all | solution.py:50
  166.9 118.1 %reduce-scatter.6.cloned.1.call-start = ((), (), s32[]{:S(2)}) async-start(), calls=%async_computation.8 | async-start | bytes 3538944 | tf_op jit(solution)/shard_map/reduce_scatter | solution.py:97
  172.5 4.1 %copy-start.6 = (bf16[512,768]{1,0:T(8,128)(2,1)S(1)}, bf16[512,768]{1,0:T(8,128)(2,1)}, u32[]{:S(2)}) copy-start(bf16[512,768]{1,0:T(8,128)(2,1)} %copy-done.5) | copy-start | bytes 2359300
  215.9 52.9 %all-to-all-start.3 = ((bf16[32,16,2048]{2,1,0:T(8,128)(2,1)}), bf16[32,16,2048]{2,1,0:T(8,128)(2,1)}, u32[]{:S(2)}, u32[]{:S(2)}) async-start(bf16[32,16,2048]{2,1,0:T(8,128)(2,1)} %bitcast.84), calls=%async_computation.3 | async-start | bytes 4194304 | tf_op jit(solution)/shard_map/all_to_all | solution.py:83
  268.8 10.2 %copy-start.3 = (f32[48,8]{1,0:T(8,128)S(1)}, f32[48,8]{1,0:T(8,128)}, u32[]{:S(2)}) copy-start(f32[48,8]{1,0:T(8,128)} %copy-done.2) | copy-start | bytes 4612
  275.7 3.3 %copy-start.1 = (bf16[384,2048]{1,0:T(8,128)(2,1)S(1)}, bf16[384,2048]{1,0:T(8,128)(2,1)}, u32[]{:S(2)}) copy-start(bf16[384,2048]{1,0:T(8,128)(2,1)} %gather_fusion) | copy-start | bytes 4718596
Sparse Core Ops, SparseCore 0:
  149.7 36.4 reduce-scatter.3
  188.7 37.6 reduce-scatter.7
  228.9 38.2 reduce-scatter.5
where the time goes:
time: 294 us; the launch traced here: 293 us
  waiting for transfers between devices  164 us (56%)
  matrix products  43.4 us (15%)
  starting transfers between devices  31.6 us (11%)
  local copies, waits for them, and re-layouts  22 us (7%)
  other arithmetic  18.5 us (6%)
  between operations  13.9 us (5%)
    all_to_all x1, waiting for transfers between devices, shards(): lax.all_to_all(outbound_grad.reshape(experts, slots, width), 'expert', sp...  44.8 us
    all_to_all x1, waiting for transfers between devices, shards(): lax.all_to_all(outbound, 'expert', split_axis=0, concat_axis=0, tiled=True)  42.9 us
    all_to_all x1, waiting for transfers between devices, shards(): lax.all_to_all(row_grad.reshape(experts, slots, width), 'expert', split_a...  40.3 us
    all_to_all x1, waiting for transfers between devices, shards(): lax.all_to_all(expert_out, 'expert', split_axis=0, concat_axis=0, tiled=T...  36 us
    dot_general x3, matrix products, contract_rows(): lax.dot_general(left, right, (((0,), (0,)), ((), ())), preferred_element_...  15.8 us
    dot_general x3, matrix products, contract_cols(): lax.dot_general(left, right, (((1,), (1,)), ((), ())), preferred_element_...  12.8 us
    all_to_all x1, starting transfers between devices, shards(): lax.all_to_all(outbound_grad.reshape(experts, slots, width), 'expert', sp...  11.9 us
    gather x1, local copies, waits for them, and re-layouts, shards(): back_grad.reshape(-1, width)[target].reshape(tok_count, top, width)  6.95 us
  transfers between devices with their start and end apart: 7, of which 4 were waited for; matrix products, arithmetic and copies ran while one was open for 19% of the time, Pallas kernels for 0%

commit v1 on v0

v1 whole, which is shorter than its diff:
```python
import jax
import jax.numpy as jnp
from jax import lax
from jax.experimental import pallas as pl
from jax.experimental.pallas import tpu as pltpu
from jax.sharding import PartitionSpec as P

MESH = pl.DeviceIdType.MESH
BF = jnp.bfloat16
F32 = jnp.float32
NZ, NY, NX = 8, 4, 4
T, C, D, F = 48, 16, 2048, 768
EXPERTS = NZ * NY
ROWS = NZ * NY * C
HD = D // 2
BACK = (7, 5, 6, 3, 4, 1, 2, 0)


def dot(a, b):
    return jnp.dot(a, b, preferred_element_type=F32)


def dot_cols(a, b):
    return lax.dot_general(a, b, (((1,), (1,)), ((), ())), preferred_element_type=F32)


def dot_rows(a, b):
    return lax.dot_general(a, b, (((0,), (0,)), ((), ())), preferred_element_type=F32)


def kernel(
    ids, probs, tok_hbm, cot_hbm, wg_hbm, wu_hbm, wd_hbm,
    layer_out, input_grad, gate_out, up_out, down_out,
    flat, ag, ai, sb, xg, eo, rback, relay, wg, wu, wd, gp, up, hid, gg, ug,
    zrecv, pg, pu, cr_a, cr_d, xh_a, xh_d, xf_a, xf_d,
    loc, ysend, yrecv, asend, arecv, isend, irecv, zsend, zrecv_sem, csend, crecv, xsend, xrecv,
):
    ex = lax.axis_index("expert")
    dp = lax.axis_index("dp")
    z, y = ex // NY, ex % NY
    x, core = dp // 2, dp % 2
    z_right = {"expert": (z + 1) % NZ * NY + y}
    z_left = {"expert": (z + NZ - 1) % NZ * NY + y}
    y_right = {"expert": z * NY + (y + 1) % NY}
    y_left = {"expert": z * NY + (y + NY - 1) % NY}
    x_right = {"dp": (x + 1) % NX * 2 + core}
    x_left = {"dp": (x + NX - 1) % NX * 2 + core}
    other = {"dp": x * 2 + 1 - core}

    started = []

    def send(src, dst, ssem, rsem, device):
        copy = pltpu.make_async_remote_copy(
            src_ref=src, dst_ref=dst, send_sem=ssem, recv_sem=rsem, device_id=device, device_id_type=MESH
        )
        copy.start()
        started.append(copy)
        return copy

    loads = {}
    for i, (src, dst) in enumerate(
        ((tok_hbm, ag.at[0, 0]), (cot_hbm, ag.at[1, 0]), (wg_hbm, wg), (wu_hbm, wu), (wd_hbm, wd))
    ):
        loads[i] = pltpu.make_async_copy(src, dst, loc.at[i])
        loads[i].start()

    barrier = pltpu.get_barrier_semaphore()
    for device in (z_right, z_left, y_right, y_left, x_right, x_left, other):
        pl.semaphore_signal(barrier, inc=1, device_id=device, device_id_type=MESH)

    flat[...] = jnp.full((128, 128), -1.0, F32)
    flat[0:T, 0:8] = ids[...].astype(F32)
    flat[0:T, 8:16] = probs[...]
    turned = flat[...].T
    expert_row = lax.broadcasted_iota(jnp.int32, (EXPERTS, 128), 0).astype(F32)
    named = jnp.zeros((EXPERTS, 128), F32)
    weight = jnp.zeros((EXPERTS, 128), F32)
    for k in range(8):
        same = turned[k : k + 1, :] == expert_row
        named = jnp.where(same, 1.0, named)
        weight = jnp.where(same, turned[8 + k : 9 + k, :], weight)
    before = (
        lax.broadcasted_iota(jnp.int32, (128, 128), 0) < lax.broadcasted_iota(jnp.int32, (128, 128), 1)
    ).astype(F32).astype(BF)
    place = jnp.where(named > 0.0, dot(named.astype(BF), before), -1.0)
    for p in range(NZ):
        ai[0, p, 0:4, :] = place[4 * p : 4 * p + 4, :]
        ai[0, p, 4:8, :] = weight[4 * p : 4 * p + 4, :]

    pl.semaphore_wait(barrier, 7)

    ag_copy = {}

    def ag_step(t, step):
        if step < 4:
            src_r, src_l = (0, 0) if step == 1 else (2 * step - 3, 2 * step - 2)
            r, l = 2 * step - 1, 2 * step
            ag_copy[t, r] = send(ag.at[t, src_r], ag.at[t, r], asend.at[t, r], arecv.at[t, r], z_right)
            ag_copy[t, l] = send(ag.at[t, src_l], ag.at[t, l], asend.at[t, l], arecv.at[t, l], z_left)
            if t == 0:
                ag_copy[2, r] = send(ai.at[src_r], ai.at[r], isend.at[r], irecv.at[r], z_right)
                ag_copy[2, l] = send(ai.at[src_l], ai.at[l], isend.at[l], irecv.at[l], z_left)
        else:
            ag_copy[t, 7] = send(
                ag.at[t, 5, :, pl.ds(0, HD)], ag.at[t, 7, :, pl.ds(0, HD)], asend.at[t, 7], arecv.at[t, 7], z_right
            )
            ag_copy[t, 0] = send(
                ag.at[t, 6, :, pl.ds(HD, HD)], ag.at[t, 7, :, pl.ds(HD, HD)], asend.at[t, 0], arecv.at[t, 0], z_left
            )
            if t == 0:
                ag_copy[2, 7] = send(ai.at[5], ai.at[7], isend.at[7], irecv.at[7], z_right)

    def ag_wait(t, slots):
        for s in slots:
            ag_copy[t, s].wait_recv()
            if s == 7:
                ag_copy[t, 0].wait_recv()
            if t == 0:
                ag_copy[2, s].wait_recv()

    def chooser(slot):
        table = ai[slot, z]
        line = lax.broadcasted_iota(jnp.int32, (8, 128), 0)
        want = lax.broadcasted_iota(jnp.int32, (C, 128), 0).astype(F32)
        picks, weights = [], []
        for r in range(NY):
            yy = (y + r) % NY
            place_row = jnp.sum(jnp.where(line == yy, table, 0.0), axis=0, keepdims=True)
            weight_row = jnp.sum(jnp.where(line == yy + 4, table, 0.0), axis=0, keepdims=True)
            hit = (place_row == want).astype(F32)
            picks.append(hit)
            weights.append(hit * weight_row)
        return jnp.concatenate(picks, axis=0), jnp.concatenate(weights, axis=0)

    y_copy = {}

    def rows(slot, r):
        return pl.ds(slot * 64 + r * C, C)

    def y_dst(t, slot, r):
        return xg.at[t, rows(slot, r)] if t < 2 else rback.at[t - 2, slot, r - 1]

    def y_src(t, slot, r):
        return sb.at[t, slot, r - 1] if t < 2 else eo.at[t - 2, rows(slot, r)]

    def y_send(t, slot):
        y_copy[t, slot, 0] = send(
            y_src(t, slot, 1), y_dst(t, slot, 3), ysend.at[t, slot, 0], yrecv.at[t, slot, 0], y_right
        )
        y_copy[t, slot, 1] = send(
            y_src(t, slot, 3), y_dst(t, slot, 1), ysend.at[t, slot, 1], yrecv.at[t, slot, 1], y_left
        )
        y_copy[t, slot, 2] = send(
            y_src(t, slot, 2), relay.at[t, slot], ysend.at[t, slot, 2], yrecv.at[t, slot, 2],
            y_right if slot % 2 == 0 else y_left,
        )

    def y_relay(t, *slots):
        for slot in slots:
            y_copy[t, slot, 2].wait_recv()
            y_copy[t, slot, 3] = send(
                relay.at[t, slot], y_dst(t, slot, 2), ysend.at[t, slot, 3], yrecv.at[t, slot, 3],
                y_right if slot % 2 == 0 else y_left,
            )

    def y_wait(t, *slots):
        for slot in slots:
            for i in (0, 1, 3):
                y_copy[t, slot, i].wait_recv()

    def select(t, *slots):
        for slot in slots:
            pick, weights = chooser(slot)
            chosen = dot(pick[:, :T].astype(BF), ag[t, slot])
            if t == 1:
                chosen = chosen * jnp.sum(weights, axis=1, keepdims=True)
            chosen = chosen.astype(BF)
            xg[t, rows(slot, 0), :] = chosen[0:C, :]
            for r in range(1, NY):
                sb[t, slot, r - 1] = chosen[r * C : (r + 1) * C, :]
            y_send(t, slot)

    def forward(c):
        band = pl.ds(c * 128, 128)

        @pl.loop(0, F // 256)
        def _(n):
            cols = pl.ds(pl.multiple_of(n * 256, 256), 256)
            g = dot(xg[0, band, :], wg[:, cols])
            u = dot(xg[0, band, :], wu[:, cols])
            gp[band, cols] = g
            up[band, cols] = u
            hid[band, cols] = (g * jax.nn.sigmoid(g) * u).astype(BF)

        @pl.loop(0, D // 256)
        def _(n):
            cols = pl.ds(pl.multiple_of(n * 256, 256), 256)
            eo[0, band, cols] = dot(hid[band, :], wd[:, cols]).astype(BF)

    def backward(c):
        band = pl.ds(c * 128, 128)

        @pl.loop(0, F // 256)
        def _(n):
            cols = pl.ds(pl.multiple_of(n * 256, 256), 256)
            hg = dot_cols(xg[1, band, :], wd[cols, :])
            g = gp[band, cols]
            s = jax.nn.sigmoid(g)
            gg[band, cols] = (hg * up[band, cols] * s * (1.0 + g * (1.0 - s))).astype(BF)
            ug[band, cols] = (hg * g * s).astype(BF)

    def row_grad(c):
        band = pl.ds(c * 128, 128)

        @pl.loop(0, D // 256)
        def _(n):
            cols = pl.ds(pl.multiple_of(n * 256, 256), 256)
            eo[1, band, cols] = (dot_cols(gg[band, :], wg[cols, :]) + dot_cols(ug[band, :], wu[cols, :])).astype(BF)

    z_copy = {}

    def combine(t, slot):
        pick, weights = chooser(slot)
        got = jnp.concatenate(
            [eo[t, rows(slot, 0), :], rback[t, slot, 0], rback[t, slot, 1], rback[t, slot, 2]], axis=0
        )
        if t == 1:
            return dot_rows(pick[:, :T].astype(BF), got)
        high = weights.astype(BF)
        low = (weights - high.astype(F32)).astype(BF)
        return dot_rows(high[:, :T], got) + dot_rows(low[:, :T], got)

    def z_step(t, slot):
        y_wait(t + 2, slot)
        total = combine(t, slot)
        if slot == 7:
            ag[t, 7] = total.astype(BF)
            z_copy[t, 0] = send(
                ag.at[t, 7, :, pl.ds(0, HD)], zrecv.at[t, 0, :, pl.ds(0, HD)],
                zsend.at[t, 0], zrecv_sem.at[t, 0], z_left,
            )
            z_copy[t, 4] = send(
                ag.at[t, 7, :, pl.ds(HD, HD)], zrecv.at[t, 0, :, pl.ds(HD, HD)],
                zsend.at[t, 4], zrecv_sem.at[t, 4], z_right,
            )
        elif slot > 0:
            leftward = slot % 2 == 1
            step = 3 - (slot - 1) // 2
            k = step if leftward else 4 + step
            z_copy[t, k - 1].wait_recv()
            if step == 1:
                half = pl.ds(0, HD) if leftward else pl.ds(HD, HD)
                lo = 0 if leftward else HD
                ag[t, slot] = total.astype(BF)
                ag[t, slot, :, half] = (total[:, lo : lo + HD] + zrecv[t, 0, :, half].astype(F32)).astype(BF)
            else:
                ag[t, slot] = (total + zrecv[t, k - 1].astype(F32)).astype(BF)
            z_copy[t, k] = send(
                ag.at[t, slot], zrecv.at[t, k], zsend.at[t, k], zrecv_sem.at[t, k], z_left if leftward else z_right
            )
        else:
            z_copy[t, 3].wait_recv()
            z_copy[t, 7].wait_recv()
            out = layer_out if t == 0 else input_grad
            out[...] = (total + zrecv[t, 3].astype(F32) + zrecv[t, 7].astype(F32)).astype(BF)

    parts = (wd, pg, pu)
    outs = (down_out, gate_out, up_out)
    deep = (F // 8, D // 8, D // 8)
    wide = (D, F, F)
    cr_of = (cr_d.at[0], cr_a.at[0], cr_a.at[1])
    xh_of = (xh_d.at[0], xh_a.at[0], xh_a.at[1])
    xf_of = (xf_d.at[0], xf_a.at[0], xf_a.at[1])
    core_copy, x_copy = {}, {}

    def band_of(w, k, c):
        return pl.multiple_of(((x + k) % NX * 2 + c) * deep[w], 32)

    def core_send(w, k):
        block = pl.ds(band_of(w, k, 1 - core), deep[w])
        core_copy[w, k] = send(
            parts[w].at[block], cr_of[w].at[k], csend.at[w, k], crecv.at[w, k], other
        )

    def wgrad_tile(w, k, c):
        grad = gg if w == 1 else ug
        start = pl.multiple_of(((x + k) % NX * 2 + c) * 256, 256)
        parts[w][pl.ds(start, 256), :] = dot_rows(xg[0, :, pl.ds(start, 256)], grad[...]).astype(BF)

    def wgrad(w, far):
        if w == 0:

            @pl.loop(0, D // 256)
            def _(n):
                cols = pl.ds(pl.multiple_of(n * 256, 256), 256)
                wd[:, cols] = dot_rows(hid[...], xg[1, :, cols]).astype(BF)

            for k in (2, 1, 3, 0):
                core_send(w, k)
        elif far:

            @pl.loop(0, NX)
            def _(k):
                wgrad_tile(w, k, 1 - core)

            for k in (2, 1, 3, 0):
                core_send(w, k)
        else:

            @pl.loop(0, NX)
            def _(k):
                wgrad_tile(w, k, core)

    def add_block(w, k, extra, finish=None):
        first = band_of(w, k, core)
        size = 32

        @pl.loop(0, deep[w] // size)
        def _(i):
            mine = pl.ds(pl.multiple_of(first + i * size, size), size)
            at = pl.ds(pl.multiple_of(i * size, size), size)
            total = parts[w][mine, :].astype(F32) + cr_of[w][k, at, :].astype(F32)
            for ref in extra:
                total = total + ref[at, :].astype(F32)
            if finish is None:
                parts[w][mine, :] = total.astype(BF)
            else:
                finish[at, :] = total

    def x_first(w):
        core_copy[w, 2].wait_recv()
        add_block(w, 2, ())
        half = wide[w] // 2
        block = pl.ds(band_of(w, 2, core), deep[w])
        x_copy[w, 0] = send(
            parts[w].at[block, pl.ds(0, half)], xh_of[w].at[0], xsend.at[w, 0], xrecv.at[w, 0], x_right
        )
        x_copy[w, 1] = send(
            parts[w].at[block, pl.ds(half, half)], xh_of[w].at[1], xsend.at[w, 1], xrecv.at[w, 1], x_left
        )

    def x_second(w):
        half = wide[w] // 2
        for i, k in ((0, 1), (1, 3)):
            core_copy[w, k].wait_recv()
            add_block(w, k, ())
            x_copy[w, i].wait_recv()
            first = band_of(w, k, core)

            @pl.loop(0, deep[w] // 32)
            def _(j):
                mine = pl.ds(pl.multiple_of(first + j * 32, 32), 32)
                at = pl.ds(pl.multiple_of(j * 32, 32), 32)
                cols = pl.ds(i * half, half)
                parts[w][mine, cols] = (
                    parts[w][mine, cols].astype(F32) + xh_of[w][i, at, :].astype(F32)
                ).astype(BF)

            x_copy[w, 2 + i] = send(
                parts[w].at[pl.ds(first, deep[w])], xf_of[w].at[i], xsend.at[w, 2 + i], xrecv.at[w, 2 + i],
                x_right if i == 0 else x_left,
            )

    def x_last(w):
        core_copy[w, 0].wait_recv()
        x_copy[w, 2].wait_recv()
        x_copy[w, 3].wait_recv()
        add_block(w, 0, (xf_of[w].at[0], xf_of[w].at[1]), outs[w])

    loads[0].wait()
    ag_step(0, 1)
    select(0, 0)
    loads[1].wait()
    select(1, 0)
    ag_wait(0, (1, 2))
    ag_step(0, 2)
    select(0, 1, 2)
    y_relay(0, 0)
    y_relay(1, 0)
    ag_wait(0, (3, 4))
    ag_step(0, 3)
    ag_step(1, 1)
    select(0, 3, 4)
    y_relay(0, 1, 2)
    ag_wait(0, (5, 6))
    ag_step(0, 4)
    select(0, 5, 6)
    ag_wait(1, (1, 2))
    ag_step(1, 2)
    y_relay(0, 3, 4)
    ag_wait(0, (7,))
    select(0, 7)
    select(1, 1, 2)
    y_relay(0, 5, 6)
    for i in (2, 3, 4):
        loads[i].wait()
    y_wait(0, 0, 1)
    forward(0)
    ag_wait(1, (3, 4))
    ag_step(1, 3)
    select(1, 3, 4)
    y_relay(0, 7)
    y_relay(1, 1, 2)
    y_wait(0, 2, 3)
    forward(1)
    ag_wait(1, (5, 6))
    ag_step(1, 4)
    select(1, 5, 6)
    y_relay(1, 3, 4)
    y_wait(0, 4, 5)
    forward(2)
    ag_wait(1, (7,))
    select(1, 7)
    y_relay(1, 5, 6)
    y_wait(0, 6, 7)
    forward(3)
    y_relay(1, 7)
    for key, copy in ag_copy.items():
        copy.wait_send()
    for s in (7, 5, 6):
        y_send(2, s)
    y_wait(1, 0, 1)
    backward(0)
    y_wait(1, 2, 3)
    backward(1)
    y_wait(1, 4, 5)
    backward(2)
    y_wait(1, 6, 7)
    backward(3)
    y_relay(2, 7)
    y_send(2, 3)
    y_send(2, 4)
    y_relay(2, 5, 6)
    wgrad(0, True)
    y_relay(2, 3)
    y_send(2, 1)
    y_send(2, 2)
    y_send(2, 0)
    y_relay(2, 4)
    z_step(0, 7)
    wgrad(1, True)
    x_first(0)
    wgrad(1, False)
    y_relay(2, 1, 2)
    z_step(0, 5)
    z_step(0, 6)
    wgrad(2, True)
    x_second(0)
    x_first(1)
    y_relay(2, 0)
    z_step(0, 3)
    z_step(0, 4)
    row_grad(3)
    row_grad(2)
    for s in (7, 5, 6):
        y_send(3, s)
    wgrad(2, False)
    z_step(0, 1)
    z_step(0, 2)
    row_grad(1)
    y_relay(3, 7)
    y_send(3, 3)
    y_send(3, 4)
    row_grad(0)
    x_second(1)
    x_first(2)
    z_step(0, 0)
    y_relay(3, 5, 6)
    for s in (1, 2, 0):
        y_send(3, s)
    x_last(0)
    z_step(1, 7)
    y_relay(3, 3, 4)
    z_step(1, 5)
    z_step(1, 6)
    x_second(2)
    y_relay(3, 1, 2)
    z_step(1, 3)
    z_step(1, 4)
    x_last(1)
    y_relay(3, 0)
    z_step(1, 1)
    z_step(1, 2)
    x_last(2)
    z_step(1, 0)

    early = [id(copy) for copy in ag_copy.values()]
    for copy in started:
        if id(copy) not in early:
            copy.wait_send()


def shards(tokens, expert_ids, gate_probs, out_cot, w_gate, w_up, w_down):
    vmem = pl.BlockSpec(memory_space=pltpu.VMEM)
    hbm = pl.BlockSpec(memory_space=pl.ANY)
    dma = pltpu.SemaphoreType.DMA
    V = pltpu.VMEM
    shape = jax.ShapeDtypeStruct
    layer_out, input_grad, gate, up, down = pl.pallas_call(
        kernel,
        out_shape=(
            shape((T, D), BF),
            shape((T, D), BF),
            shape((D // 8, F), F32),
            shape((D // 8, F), F32),
            shape((F // 8, D), F32),
        ),
        in_specs=[vmem, vmem, hbm, hbm, hbm, hbm, hbm],
        out_specs=(vmem,) * 5,
        scratch_shapes=[
            V((128, 128), F32),
            V((2, NZ, T, D), BF),
            V((NZ, NZ, 8, 128), F32),
            V((2, NZ, 3, C, D), BF),
            V((2, ROWS, D), BF),
            V((2, ROWS, D), BF),
            V((2, NZ, 3, C, D), BF),
            V((4, NZ, C, D), BF),
            V((D, F), BF),
            V((D, F), BF),
            V((F, D), BF),
            V((ROWS, F), F32),
            V((ROWS, F), F32),
            V((ROWS, F), BF),
            V((ROWS, F), BF),
            V((ROWS, F), BF),
            V((2, NZ, T, D), BF),
            V((D, F), BF),
            V((D, F), BF),
            V((2, NX, D // 8, F), BF),
            V((1, NX, F // 8, D), BF),
            V((2, 2, D // 8, F // 2), BF),
            V((1, 2, F // 8, D // 2), BF),
            V((2, 2, D // 8, F), BF),
            V((1, 2, F // 8, D), BF),
            dma((5,)),
            dma((4, NZ, 4)),
            dma((4, NZ, 4)),
            dma((2, NZ)),
            dma((2, NZ)),
            dma((NZ,)),
            dma((NZ,)),
            dma((2, 8)),
            dma((2, 8)),
            dma((3, NX)),
            dma((3, NX)),
            dma((3, 4)),
            dma((3, 4)),
        ],
        compiler_params=pltpu.CompilerParams(
            collective_id=0, has_side_effects=True, vmem_limit_bytes=66_900_000
        ),
        name="expert_layer",
    )(expert_ids, gate_probs, tokens, out_cot, w_gate[0], w_up[0], w_down[0])
    return (layer_out, input_grad, gate[None], up[None], down[None])


def solution(mesh):
    placed = (
        P(("dp", "expert"), None),
        P(("dp", "expert"), None),
        P(("dp", "expert"), None),
        P(("dp", "expert"), None),
        P("expert", None, None),
        P("expert", None, None),
        P("expert", None, None),
    )
    return jax.shard_map(
        shards,
        mesh=mesh,
        in_specs=placed,
        out_specs=(
            P(("dp", "expert"), None),
            P(("dp", "expert"), None),
            P("expert", "dp", None),
            P("expert", "dp", None),
            P("expert", "dp", None),
        ),
        check_vma=False,
    )
```

time: 294 us -> 149 us (0.51)
  waiting for transfers between devices: 164 us -> 0 us
  Pallas kernels: 0 us -> 137 us
  matrix products: 43.4 us -> 0 us
  starting transfers between devices: 31.6 us -> 0 us
  other arithmetic: 18.5 us -> 0 us
  between operations: 13.9 us -> 0.65 us
  local copies, waits for them, and re-layouts: 22 us -> 11.1 us
    all_to_all x4 -> x0, waiting for transfers between devices: 164 us -> none  [the longest x1 44.8 us: shards(): lax.all_to_all(outbound_grad.reshape(experts, slots, width), 'expert', sp...]
    pallas_call x0 -> x1, Pallas kernels: none -> 137 us  [shards(): pl.pallas_call(kernel, out_shape=(shape((T, D), BF), shape((T, D), BF), s...]
    dot_general x9 -> x0, matrix products: 43.4 us -> none  [the longest x3 15.8 us: contract_rows(): lax.dot_general(left, right, (((0,), (0,)), ((), ())), preferred_element_...]
    all_to_all x4 -> x0, starting transfers between devices: 31 us -> none  [the longest x1 11.9 us: shards(): lax.all_to_all(outbound_grad.reshape(experts, slots, width), 'expert', sp...]
    gather x2 -> x0, local copies, waits for them, and re-layouts: 13.9 us -> none  [the longest x1 6.95 us: shards(): back_grad.reshape(-1, width)[target].reshape(tok_count, top, width)]
    unnamed x18 -> x9, local copies, waits for them, and re-layouts: 3.07 us -> 11.1 us
    broadcast_in_dim x3 -> x0, other arithmetic: 5.8 us -> none  [the longest x1 1.94 us: shards(): down_grad[None]]
    reduce_sum x3 -> x0, other arithmetic: 5.47 us -> none  [the longest x1 3.27 us: shards(): jnp.sum(gathered.astype(jnp.float32), axis=1).astype(jnp.bfloat16)]
  transfers between devices with their start and end apart: 7 -> 0, of which waited for: 4 -> 0; matrix products, arithmetic and copies ran while one was open for 19% -> 0% of each run, Pallas kernels for 0% -> 0%
where the time goes in v1:
time: 149 us
  Pallas kernels  137 us (92%)
  local copies, waits for them, and re-layouts  11.1 us (7%)
    pallas_call x1, Pallas kernels, shards(): pl.pallas_call(kernel, out_shape=(shape((T, D), BF), shape((T, D), BF), s...  137 us
    unnamed x9, local copies, waits for them, and re-layouts  11.1 us

profile of v1, /device:TPU:8, one launch (start us, length us, event | category | flops | bytes accessed | tf_op | source)
XLA Modules:
  0.0 148.5 jit_solution(1499473546464879971)
XLA Ops:
  0.6 1.4 copy.12.ids
  2.0 1.4 copy.13.probs
  3.4 136.8 %expert_layer.1 = (bf16[48,2048]{1,0:T(8,128)(2,1)}, bf16[48,2048]{1,0:T(8,128)(2,1)}, f32[256,768]{1,0:T(8,128)}, f32[256,768]{1,0:T(8,128)}, f32[96,2048]{1,0:T(8,128)}) custom-call(s32[48,8]{1,0:T(8,128)} %copy.12.ids, f32[48,8]{1,0:T(8,128)} %copy.13.probs, bf16[48,2048]{1,0:T(8,128)(2,1)} %tok_hbm.1, bf16[48,2048]{1,0:T(8,128)(2,1)} %cot_hbm.1, ...), custom_call_target="tpu_custom_call" | custom-call | tf_op jit(solution)/shard_map/expert_layer/pallas_call | solution.py:499
  140.2 0.0 copy-start
  140.2 1.7 %copy.19 = bf16[48,2048]{1,0:T(8,128)(2,1)} copy(bf16[48,2048]{1,0:T(8,128)(2,1)} %get-tuple-element.20) | data formatting | bytes 393216
  141.9 1.6 %copy.20 = bf16[48,2048]{1,0:T(8,128)(2,1)} copy(bf16[48,2048]{1,0:T(8,128)(2,1)} %get-tuple-element.21) | data formatting | bytes 393216
  143.5 2.1 %copy.21 = f32[1,256,768]{2,1,0:T(8,128)} copy(f32[1,256,768]{2,1,0:T(8,128)} %bitcast.11) | data formatting | bytes 1572864
  145.6 2.1 %copy.22 = f32[1,256,768]{2,1,0:T(8,128)} copy(f32[1,256,768]{2,1,0:T(8,128)} %bitcast.10) | data formatting | bytes 1572864
  147.6 0.0 copy-done
  147.6 0.9 copy.23
Async XLA Ops:
  140.2 7.4 %copy-start = (f32[96,2048]{1,0:T(8,128)S(1)}, f32[96,2048]{1,0:T(8,128)}, u32[]{:S(2)}) copy-start(f32[96,2048]{1,0:T(8,128)} %get-tuple-element.14) | copy-start | bytes 2359300

commit v2 on v1

--- a/solution.py
+++ b/solution.py
@@ -29,9 +29,9 @@
 
 
 def kernel(
-    ids, probs, tok_hbm, cot_hbm, wg_hbm, wu_hbm, wd_hbm,
+    ids_hbm, probs_hbm, tok_hbm, cot_hbm, wg_hbm, wu_hbm, wd_hbm,
     layer_out, input_grad, gate_out, up_out, down_out,
-    flat, ag, ai, sb, xg, eo, rback, relay, wg, wu, wd, gp, up, hid, gg, ug,
+    ids, probs, ag, ai, sb, xg, eo, rback, relay, wg, wu, wd, gp, up, hid, gg, ug,
     zrecv, pg, pu, cr_a, cr_d, xh_a, xh_d, xf_a, xf_d,
     loc, ysend, yrecv, asend, arecv, isend, irecv, zsend, zrecv_sem, csend, crecv, xsend, xrecv,
 ):
@@ -59,7 +59,10 @@
 
     loads = {}
     for i, (src, dst) in enumerate(
-        ((tok_hbm, ag.at[0, 0]), (cot_hbm, ag.at[1, 0]), (wg_hbm, wg), (wu_hbm, wu), (wd_hbm, wd))
+        (
+            (ids_hbm, ids), (probs_hbm, probs), (tok_hbm, ag.at[0, 0]), (cot_hbm, ag.at[1, 0]),
+            (wg_hbm, wg), (wu_hbm, wu), (wd_hbm, wd),
+        )
     ):
         loads[i] = pltpu.make_async_copy(src, dst, loc.at[i])
         loads[i].start()
@@ -68,17 +71,18 @@
     for device in (z_right, z_left, y_right, y_left, x_right, x_left, other):
         pl.semaphore_signal(barrier, inc=1, device_id=device, device_id_type=MESH)
 
-    flat[...] = jnp.full((128, 128), -1.0, F32)
-    flat[0:T, 0:8] = ids[...].astype(F32)
-    flat[0:T, 8:16] = probs[...]
-    turned = flat[...].T
-    expert_row = lax.broadcasted_iota(jnp.int32, (EXPERTS, 128), 0).astype(F32)
+    loads[0].wait()
+    loads[1].wait()
+    fill = jnp.full((8, 128 - T), -1, jnp.int32)
+    chosen_ids = jnp.concatenate([ids[...], fill], axis=1)
+    chosen_probs = jnp.concatenate([probs[...], fill.astype(F32)], axis=1)
+    expert_row = lax.broadcasted_iota(jnp.int32, (EXPERTS, 128), 0)
     named = jnp.zeros((EXPERTS, 128), F32)
     weight = jnp.zeros((EXPERTS, 128), F32)
     for k in range(8):
-        same = turned[k : k + 1, :] == expert_row
+        same = chosen_ids[k : k + 1, :] == expert_row
         named = jnp.where(same, 1.0, named)
-        weight = jnp.where(same, turned[8 + k : 9 + k, :], weight)
+        weight = jnp.where(same, chosen_probs[k : k + 1, :], weight)
     before = (
         lax.broadcasted_iota(jnp.int32, (128, 128), 0) < lax.broadcasted_iota(jnp.int32, (128, 128), 1)
     ).astype(F32).astype(BF)
@@ -88,6 +92,8 @@
         ai[0, p, 4:8, :] = weight[4 * p : 4 * p + 4, :]
 
     pl.semaphore_wait(barrier, 7)
+
+    loaded = set()
 
     ag_copy = {}
 
@@ -110,13 +116,28 @@
             if t == 0:
                 ag_copy[2, 7] = send(ai.at[5], ai.at[7], isend.at[7], irecv.at[7], z_right)
 
+    seen = set()
+
+    def once(t, s):
+        if (t, s) not in seen:
+            seen.add((t, s))
+            ag_copy[t, s].wait_recv()
+
     def ag_wait(t, slots):
         for s in slots:
-            ag_copy[t, s].wait_recv()
+            once(t, s)
             if s == 7:
-                ag_copy[t, 0].wait_recv()
-            if t == 0:
-                ag_copy[2, s].wait_recv()
+                once(t, 0)
+            once(2, s)
+
+    def gather(t, step):
+        if step == 1:
+            if t not in loaded:
+                loads[2 + t].wait()
+                loaded.add(t)
+        else:
+            ag_wait(t, (2 * step - 3, 2 * step - 2))
+        ag_step(t, step)
 
     def chooser(slot):
         table = ai[slot, z]
@@ -168,19 +189,29 @@
             for i in (0, 1, 3):
                 y_copy[t, slot, i].wait_recv()
 
-    def select(t, *slots):
-        for slot in slots:
-            pick, weights = chooser(slot)
-            chosen = dot(pick[:, :T].astype(BF), ag[t, slot])
-            if t == 1:
-                chosen = chosen * jnp.sum(weights, axis=1, keepdims=True)
-            chosen = chosen.astype(BF)
-            xg[t, rows(slot, 0), :] = chosen[0:C, :]
-            for r in range(1, NY):
-                sb[t, slot, r - 1] = chosen[r * C : (r + 1) * C, :]
-            y_send(t, slot)
+    def choose(t, slot):
+        if slot > 0:
+            ag_wait(t, (slot,))
+        elif t not in loaded:
+            loads[2 + t].wait()
+            loaded.add(t)
+        pick, weights = chooser(slot)
+        chosen = dot(pick[:, :T].astype(BF), ag[t, slot])
+        if t == 1:
+            chosen = chosen * jnp.sum(weights, axis=1, keepdims=True)
+        chosen = chosen.astype(BF)
+        xg[t, rows(slot, 0), :] = chosen[0:C, :]
+        for r in range(1, NY):
+            sb[t, slot, r - 1] = chosen[r * C : (r + 1) * C, :]
+        y_send(t, slot)
+
+    down_ready = []
 
     def forward(c):
+        y_wait(0, 2 * c, 2 * c + 1)
+        if c == 0:
+            loads[4].wait()
+            loads[5].wait()
         band = pl.ds(c * 128, 128)
 
         @pl.loop(0, F // 256)
@@ -192,12 +223,22 @@
             up[band, cols] = u
             hid[band, cols] = (g * jax.nn.sigmoid(g) * u).astype(BF)
 
+    def down(c):
+        if not down_ready:
+            loads[6].wait()
+            down_ready.append(c)
+        band = pl.ds(c * 128, 128)
+
         @pl.loop(0, D // 256)
         def _(n):
             cols = pl.ds(pl.multiple_of(n * 256, 256), 256)
             eo[0, band, cols] = dot(hid[band, :], wd[:, cols]).astype(BF)
 
     def backward(c):
+        y_wait(1, 2 * c, 2 * c + 1)
+        if not down_ready:
+            loads[6].wait()
+            down_ready.append(c)
         band = pl.ds(c * 128, 128)
 
         @pl.loop(0, F // 256)
@@ -234,6 +275,9 @@
         y_wait(t + 2, slot)
         total = combine(t, slot)
         if slot == 7:
+            for key, copy in ag_copy.items():
+                if key[0] == t:
+                    copy.wait_send()
             ag[t, 7] = total.astype(BF)
             z_copy[t, 0] = send(
                 ag.at[t, 7, :, pl.ds(0, HD)], zrecv.at[t, 0, :, pl.ds(0, HD)],
@@ -339,27 +383,27 @@
             parts[w].at[block, pl.ds(half, half)], xh_of[w].at[1], xsend.at[w, 1], xrecv.at[w, 1], x_left
         )
 
-    def x_second(w):
+    def x_second(w, i):
         half = wide[w] // 2
-        for i, k in ((0, 1), (1, 3)):
-            core_copy[w, k].wait_recv()
-            add_block(w, k, ())
-            x_copy[w, i].wait_recv()
-            first = band_of(w, k, core)
-
-            @pl.loop(0, deep[w] // 32)
-            def _(j):
-                mine = pl.ds(pl.multiple_of(first + j * 32, 32), 32)
-                at = pl.ds(pl.multiple_of(j * 32, 32), 32)
-                cols = pl.ds(i * half, half)
-                parts[w][mine, cols] = (
-                    parts[w][mine, cols].astype(F32) + xh_of[w][i, at, :].astype(F32)
-                ).astype(BF)
-
-            x_copy[w, 2 + i] = send(
-                parts[w].at[pl.ds(first, deep[w])], xf_of[w].at[i], xsend.at[w, 2 + i], xrecv.at[w, 2 + i],
-                x_right if i == 0 else x_left,
-            )
+        k = (1, 3)[i]
+        core_copy[w, k].wait_recv()
+        add_block(w, k, ())
+        x_copy[w, i].wait_recv()
+        first = band_of(w, k, core)
+
+        @pl.loop(0, deep[w] // 32)
+        def _(j):
+            mine = pl.ds(pl.multiple_of(first + j * 32, 32), 32)
+            at = pl.ds(pl.multiple_of(j * 32, 32), 32)
+            cols = pl.ds(i * half, half)
+            parts[w][mine, cols] = (
+                parts[w][mine, cols].astype(F32) + xh_of[w][i, at, :].astype(F32)
+            ).astype(BF)
+
+        x_copy[w, 2 + i] = send(
+            parts[w].at[pl.ds(first, deep[w])], xf_of[w].at[i], xsend.at[w, 2 + i], xrecv.at[w, 2 + i],
+            x_right if i == 0 else x_left,
+        )
 
     def x_last(w):
         core_copy[w, 0].wait_recv()
@@ -367,127 +411,41 @@
         x_copy[w, 3].wait_recv()
         add_block(w, 0, (xf_of[w].at[0], xf_of[w].at[1]), outs[w])
 
-    loads[0].wait()
-    ag_step(0, 1)
-    select(0, 0)
-    loads[1].wait()
-    select(1, 0)
-    ag_wait(0, (1, 2))
-    ag_step(0, 2)
-    select(0, 1, 2)
-    y_relay(0, 0)
-    y_relay(1, 0)
-    ag_wait(0, (3, 4))
-    ag_step(0, 3)
-    ag_step(1, 1)
-    select(0, 3, 4)
-    y_relay(0, 1, 2)
-    ag_wait(0, (5, 6))
-    ag_step(0, 4)
-    select(0, 5, 6)
-    ag_wait(1, (1, 2))
-    ag_step(1, 2)
-    y_relay(0, 3, 4)
-    ag_wait(0, (7,))
-    select(0, 7)
-    select(1, 1, 2)
-    y_relay(0, 5, 6)
-    for i in (2, 3, 4):
-        loads[i].wait()
-    y_wait(0, 0, 1)
-    forward(0)
-    ag_wait(1, (3, 4))
-    ag_step(1, 3)
-    select(1, 3, 4)
-    y_relay(0, 7)
-    y_relay(1, 1, 2)
-    y_wait(0, 2, 3)
-    forward(1)
-    ag_wait(1, (5, 6))
-    ag_step(1, 4)
-    select(1, 5, 6)
-    y_relay(1, 3, 4)
-    y_wait(0, 4, 5)
-    forward(2)
-    ag_wait(1, (7,))
-    select(1, 7)
-    y_relay(1, 5, 6)
-    y_wait(0, 6, 7)
-    forward(3)
-    y_relay(1, 7)
-    for key, copy in ag_copy.items():
-        copy.wait_send()
-    for s in (7, 5, 6):
-        y_send(2, s)
-    y_wait(1, 0, 1)
-    backward(0)
-    y_wait(1, 2, 3)
-    backward(1)
-    y_wait(1, 4, 5)
-    backward(2)
-    y_wait(1, 6, 7)
-    backward(3)
-    y_relay(2, 7)
-    y_send(2, 3)
-    y_send(2, 4)
-    y_relay(2, 5, 6)
-    wgrad(0, True)
-    y_relay(2, 3)
-    y_send(2, 1)
-    y_send(2, 2)
-    y_send(2, 0)
-    y_relay(2, 4)
-    z_step(0, 7)
-    wgrad(1, True)
-    x_first(0)
-    wgrad(1, False)
-    y_relay(2, 1, 2)
-    z_step(0, 5)
-    z_step(0, 6)
-    wgrad(2, True)
-    x_second(0)
-    x_first(1)
-    y_relay(2, 0)
-    z_step(0, 3)
-    z_step(0, 4)
-    row_grad(3)
-    row_grad(2)
-    for s in (7, 5, 6):
-        y_send(3, s)
-    wgrad(2, False)
-    z_step(0, 1)
-    z_step(0, 2)
-    row_grad(1)
-    y_relay(3, 7)
-    y_send(3, 3)
-    y_send(3, 4)
-    row_grad(0)
-    x_second(1)
-    x_first(2)
-    z_step(0, 0)
-    y_relay(3, 5, 6)
-    for s in (1, 2, 0):
-        y_send(3, s)
-    x_last(0)
-    z_step(1, 7)
-    y_relay(3, 3, 4)
-    z_step(1, 5)
-    z_step(1, 6)
-    x_second(2)
-    y_relay(3, 1, 2)
-    z_step(1, 3)
-    z_step(1, 4)
-    x_last(1)
-    y_relay(3, 0)
-    z_step(1, 1)
-    z_step(1, 2)
-    x_last(2)
-    z_step(1, 0)
-
-    early = [id(copy) for copy in ag_copy.values()]
+    for step in (
+        (gather, 0, 1), (choose, 1, 0), (gather, 1, 1), (choose, 0, 0), (choose, 0, 2), (gather, 0, 2),
+        (choose, 0, 1), (choose, 1, 1), (gather, 1, 2), (y_relay, 0, 0), (y_relay, 0, 1), (choose, 1, 2),
+        (choose, 0, 3), (y_relay, 1, 0), (gather, 0, 3), (forward, 0), (y_relay, 0, 2), (y_relay, 1, 1),
+        (choose, 0, 4), (choose, 1, 3), (choose, 1, 4), (gather, 0, 4), (gather, 1, 3), (y_relay, 0, 3),
+        (backward, 0), (choose, 0, 5), (row_grad, 0), (choose, 0, 6), (y_relay, 1, 2), (y_relay, 0, 4),
+        (y_relay, 1, 4), (y_relay, 1, 3), (forward, 1), (down, 0), (y_relay, 0, 5), (choose, 0, 7), (gather, 1, 4),
+        (y_relay, 0, 6), (choose, 1, 5), (backward, 1), (row_grad, 1), (y_relay, 0, 7), (choose, 1, 7), (down, 1),
+        (choose, 1, 6), (y_relay, 1, 5), (forward, 2), (forward, 3), (y_relay, 1, 7), (down, 2), (y_relay, 1, 6),
+        (y_send, 2, 4), (down, 3), (y_send, 2, 7), (backward, 2), (y_send, 2, 6), (backward, 3), (y_send, 2, 5),
+        (wgrad, 1, 1), (row_grad, 3), (y_send, 3, 7), (wgrad, 1, 0), (y_send, 3, 6), (y_send, 2, 3), (y_relay, 2, 7),
+        (x_first, 1), (y_relay, 2, 6), (wgrad, 2, 1), (row_grad, 2), (y_relay, 3, 7), (wgrad, 2, 0),
+        (x_second, 1, 0), (y_send, 3, 5), (y_relay, 2, 5), (x_second, 1, 1), (y_send, 3, 4), (wgrad, 0, 1),
+        (y_send, 2, 2), (y_relay, 3, 6), (z_step, 0, 7), (y_relay, 3, 5), (y_send, 3, 3), (y_relay, 2, 3),
+        (z_step, 1, 7), (x_first, 0), (z_step, 0, 6), (z_step, 0, 5), (y_send, 2, 1), (x_first, 2), (x_last, 1),
+        (y_relay, 2, 4), (y_relay, 3, 4), (z_step, 1, 6), (z_step, 1, 5), (y_relay, 2, 2), (x_second, 0, 0),
+        (x_second, 0, 1), (y_relay, 3, 3), (y_send, 2, 0), (z_step, 0, 3), (y_send, 3, 1), (z_step, 0, 4),
+        (y_relay, 2, 1), (y_send, 3, 2), (x_second, 2, 1), (z_step, 1, 4), (z_step, 1, 3), (y_relay, 2, 0),
+        (z_step, 0, 2), (y_relay, 3, 1), (y_send, 3, 0), (y_relay, 3, 2), (x_second, 2, 0), (z_step, 0, 1),
+        (z_step, 1, 1), (y_relay, 3, 0), (x_last, 0), (z_step, 1, 2), (z_step, 0, 0), (x_last, 2), (z_step, 1, 0),
+    ):
+        step[0](*step[1:])
+
+    early = [id(copy) for key, copy in ag_copy.items() if key[0] < 2]
     for copy in started:
         if id(copy) not in early:
             copy.wait_send()
+
+
+def store(*refs):
+    copies = [pltpu.make_async_copy(refs[i], refs[5 + i], refs[10].at[i]) for i in range(5)]
+    for copy in copies:
+        copy.start()
+    for copy in copies:
+        copy.wait()
 
 
 def shards(tokens, expert_ids, gate_probs, out_cot, w_gate, w_up, w_down):
@@ -495,20 +453,20 @@
     hbm = pl.BlockSpec(memory_space=pl.ANY)
     dma = pltpu.SemaphoreType.DMA
     V = pltpu.VMEM
-    shape = jax.ShapeDtypeStruct
-    layer_out, input_grad, gate, up, down = pl.pallas_call(
+    results = pl.pallas_call(
         kernel,
         out_shape=(
-            shape((T, D), BF),
-            shape((T, D), BF),
-            shape((D // 8, F), F32),
-            shape((D // 8, F), F32),
-            shape((F // 8, D), F32),
+            V((T, D), BF),
+            V((T, D), BF),
+            V((D // 8, F), F32),
+            V((D // 8, F), F32),
+            V((F // 8, D), F32),
         ),
-        in_specs=[vmem, vmem, hbm, hbm, hbm, hbm, hbm],
+        in_specs=[hbm] * 7,
         out_specs=(vmem,) * 5,
         scratch_shapes=[
-            V((128, 128), F32),
+            V((8, T), jnp.int32),
+            V((8, T), F32),
             V((2, NZ, T, D), BF),
             V((NZ, NZ, 8, 128), F32),
             V((2, NZ, 3, C, D), BF),
@@ -533,7 +491,7 @@
             V((1, 2, F // 8, D // 2), BF),
             V((2, 2, D // 8, F), BF),
             V((1, 2, F // 8, D), BF),
-            dma((5,)),
+            dma((7,)),
             dma((4, NZ, 4)),
             dma((4, NZ, 4)),
             dma((2, NZ)),
@@ -548,10 +506,19 @@
             dma((3, 4)),
         ],
         compiler_params=pltpu.CompilerParams(
-            collective_id=0, has_side_effects=True, vmem_limit_bytes=66_900_000
+            collective_id=0, has_side_effects=True, vmem_limit_bytes=63_900_000
         ),
         name="expert_layer",
-    )(expert_ids, gate_probs, tokens, out_cot, w_gate[0], w_up[0], w_down[0])
+    )(expert_ids.T, gate_probs.T, tokens, out_cot, w_gate[0], w_up[0], w_down[0])
+    layer_out, input_grad, gate, up, down = pl.pallas_call(
+        store,
+        out_shape=tuple(jax.ShapeDtypeStruct(r.shape, r.dtype) for r in results),
+        in_specs=[hbm] * 5,
+        out_specs=(hbm,) * 5,
+        scratch_shapes=[dma((5,))],
+        compiler_params=pltpu.CompilerParams(vmem_limit_bytes=1 << 20),
+        name="store",
+    )(*results)
     return (layer_out, input_grad, gate[None], up[None], down[None])
 
 

time: 149 us -> 119 us (0.80)
  Pallas kernels: 137 us -> 117 us
  local copies, waits for them, and re-layouts: 11.1 us -> 0 us
    pallas_call x1 -> x2, Pallas kernels: 137 us -> 117 us  [the longest x1 115 us: shards(): pl.pallas_call(kernel, out_shape=(V((T, D), BF), V((T, D), BF), V((D // 8...]
    unnamed x9 -> x0, local copies, waits for them, and re-layouts: 11.1 us -> none
where the time goes in v2:
time: 119 us; the launch traced here: 117 us
  Pallas kernels  117 us (98%)
    pallas_call x1, Pallas kernels, shards(): pl.pallas_call(kernel, out_shape=(V((T, D), BF), V((T, D), BF), V((D // 8...  115 us

profile of v2, /device:TPU:8, one launch (start us, length us, event | category | flops | bytes accessed | tf_op | source)
XLA Modules:
  0.0 117.2 jit_solution(6169142350475563545)
XLA Ops:
  0.6 115.0 %expert_layer.1 = (bf16[48,2048]{1,0:T(8,128)(2,1)S(1)}, bf16[48,2048]{1,0:T(8,128)(2,1)S(1)}, f32[256,768]{1,0:T(8,128)S(1)}, f32[256,768]{1,0:T(8,128)S(1)}, f32[96,2048]{1,0:T(8,128)S(1)}) custom-call(s32[8,48]{1,0:T(8,128)} %bitcast.11, f32[8,48]{1,0:T(8,128)} %bitcast.12, bf16[48,2048]{1,0:T(8,128)(2,1)} %tok_hbm.1, bf16[48,2048]{1,0:T(8,128)(2,1)} %cot_hbm.1, ...), custom_call_target="tpu_custom_call" | custom-call | tf_op jit(solution)/shard_map/expert_layer/pallas_call | solution.py:456
  115.6 1.6 %store.1 = (bf16[48,2048]{1,0:T(8,128)(2,1)}, bf16[48,2048]{1,0:T(8,128)(2,1)}, f32[256,768]{1,0:T(8,128)}, f32[256,768]{1,0:T(8,128)}, f32[96,2048]{1,0:T(8,128)}) custom-call(bf16[48,2048]{1,0:T(8,128)(2,1)S(1)} %get-tuple-element.15.refs_0_, bf16[48,2048]{1,0:T(8,128)(2,1)S(1)} %get-tuple-element.16.refs_1_, f32[256,768]{1,0:T(8,128)S(1)} %get-tuple-element.17.refs_2_, ...), custom_call_target="tpu_custom_call" | custom-call | tf_op jit(solution)/shard_map/store/pallas_call | solution.py:513

commit v3 on v2

--- a/solution.py
+++ b/solution.py
@@ -31,9 +31,10 @@
 def kernel(
     ids_hbm, probs_hbm, tok_hbm, cot_hbm, wg_hbm, wu_hbm, wd_hbm,
     layer_out, input_grad, gate_out, up_out, down_out,
-    ids, probs, ag, ai, sb, xg, eo, rback, relay, wg, wu, wd, gp, up, hid, gg, ug,
+    ids, probs, chooser_rows, far_send, far_relay, far_info, drelay, dland, ag, ai, sb, xg, eo, rback, relay, wg, wu, wd, gp, up, hid, gg, ug,
     zrecv, pg, pu, cr_a, cr_d, xh_a, xh_d, xf_a, xf_d,
-    loc, ysend, yrecv, asend, arecv, isend, irecv, zsend, zrecv_sem, csend, crecv, xsend, xrecv,
+    loc, ysend, yrecv, asend, arecv, isend, irecv, zsend, zrecv_sem, csend, crecv, xsend, xrecv, fsend, frecv,
+    dsend, drecv,
 ):
     ex = lax.axis_index("expert")
     dp = lax.axis_index("dp")
@@ -41,12 +42,18 @@
     x, core = dp // 2, dp % 2
     z_right = {"expert": (z + 1) % NZ * NY + y}
     z_left = {"expert": (z + NZ - 1) % NZ * NY + y}
+    z_right2 = {"expert": (z + 2) % NZ * NY + y}
+    z_left2 = {"expert": (z + NZ - 2) % NZ * NY + y}
     y_right = {"expert": z * NY + (y + 1) % NY}
     y_left = {"expert": z * NY + (y + NY - 1) % NY}
     x_right = {"dp": (x + 1) % NX * 2 + core}
     x_left = {"dp": (x + NX - 1) % NX * 2 + core}
     other = {"dp": x * 2 + 1 - core}
 
+    def line_of(table, index):
+        line = lax.broadcasted_iota(jnp.int32, (8, 128), 0)
+        return jnp.sum(jnp.where(line == index, table, 0.0), axis=0, keepdims=True)
+
     started = []
 
     def send(src, dst, ssem, rsem, device):
@@ -68,7 +75,7 @@
         loads[i].start()
 
     barrier = pltpu.get_barrier_semaphore()
-    for device in (z_right, z_left, y_right, y_left, x_right, x_left, other):
+    for device in (z_right, z_left, z_right2, z_left2, y_right, y_left, x_right, x_left, other):
         pl.semaphore_signal(barrier, inc=1, device_id=device, device_id_type=MESH)
 
     loads[0].wait()
@@ -91,7 +98,13 @@
         ai[0, p, 0:4, :] = place[4 * p : 4 * p + 4, :]
         ai[0, p, 4:8, :] = weight[4 * p : 4 * p + 4, :]
 
-    pl.semaphore_wait(barrier, 7)
+    for i, shift in enumerate((0, 1, NZ - 1, 2, NZ - 2)):
+        table = ai[0, (z + shift) % NZ]
+        far_send[2 * i : 2 * i + 1, :] = line_of(table, (y + 2) % NY)
+        far_send[2 * i + 1 : 2 * i + 2, :] = line_of(table, (y + 2) % NY + 4)
+    far_send[10:16, :] = jnp.zeros((6, 128), F32)
+
+    pl.semaphore_wait(barrier, 9)
 
     loaded = set()
 
@@ -139,19 +152,21 @@
             ag_wait(t, (2 * step - 3, 2 * step - 2))
         ag_step(t, step)
 
+    cached = set()
+
+    def place_rows(place_row, weight_row):
+        want = lax.broadcasted_iota(jnp.int32, (C, 128), 0).astype(F32)
+        return jnp.where(place_row == want, weight_row, 0.0)
+
     def chooser(slot):
-        table = ai[slot, z]
-        line = lax.broadcasted_iota(jnp.int32, (8, 128), 0)
-        want = lax.broadcasted_iota(jnp.int32, (C, 128), 0).astype(F32)
-        picks, weights = [], []
-        for r in range(NY):
-            yy = (y + r) % NY
-            place_row = jnp.sum(jnp.where(line == yy, table, 0.0), axis=0, keepdims=True)
-            weight_row = jnp.sum(jnp.where(line == yy + 4, table, 0.0), axis=0, keepdims=True)
-            hit = (place_row == want).astype(F32)
-            picks.append(hit)
-            weights.append(hit * weight_row)
-        return jnp.concatenate(picks, axis=0), jnp.concatenate(weights, axis=0)
+        if slot not in cached:
+            cached.add(slot)
+            table = ai[slot, z]
+            for r in range(NY):
+                yy = (y + r) % NY
+                chooser_rows[slot, r * C : (r + 1) * C, :] = place_rows(line_of(table, yy), line_of(table, yy + 4))
+        weights = chooser_rows[slot]
+        return (weights > 0.0).astype(F32), weights
 
     y_copy = {}
 
@@ -163,6 +178,12 @@
 
     def y_src(t, slot, r):
         return sb.at[t, slot, r - 1] if t < 2 else eo.at[t - 2, rows(slot, r)]
+
+    def crosses(t, slot):
+        return t < 2 or slot >= 5
+
+    def relay_side(t, slot):
+        return y_right if (slot + (t if slot == 7 and t >= 2 else 0)) % 2 == 0 else y_left
 
     def y_send(t, slot):
         y_copy[t, slot, 0] = send(
@@ -171,23 +192,22 @@
         y_copy[t, slot, 1] = send(
             y_src(t, slot, 3), y_dst(t, slot, 1), ysend.at[t, slot, 1], yrecv.at[t, slot, 1], y_left
         )
-        y_copy[t, slot, 2] = send(
-            y_src(t, slot, 2), relay.at[t, slot], ysend.at[t, slot, 2], yrecv.at[t, slot, 2],
-            y_right if slot % 2 == 0 else y_left,
-        )
-
-    def y_relay(t, *slots):
-        for slot in slots:
-            y_copy[t, slot, 2].wait_recv()
-            y_copy[t, slot, 3] = send(
-                relay.at[t, slot], y_dst(t, slot, 2), ysend.at[t, slot, 3], yrecv.at[t, slot, 3],
-                y_right if slot % 2 == 0 else y_left,
-            )
+        if crosses(t, slot):
+            y_copy[t, slot, 2] = send(
+                y_src(t, slot, 2), relay.at[t, slot], ysend.at[t, slot, 2], yrecv.at[t, slot, 2], relay_side(t, slot)
+            )
+
+    def y_relay(t, slot):
+        y_copy[t, slot, 2].wait_recv()
+        y_copy[t, slot, 3] = send(
+            relay.at[t, slot], y_dst(t, slot, 2), ysend.at[t, slot, 3], yrecv.at[t, slot, 3], relay_side(t, slot)
+        )
 
     def y_wait(t, *slots):
         for slot in slots:
             for i in (0, 1, 3):
-                y_copy[t, slot, i].wait_recv()
+                if i < 3 or crosses(t, slot):
+                    y_copy[t, slot, i].wait_recv()
 
     def choose(t, slot):
         if slot > 0:
@@ -260,24 +280,78 @@
 
     z_copy = {}
 
-    def combine(t, slot):
-        pick, weights = chooser(slot)
-        got = jnp.concatenate(
-            [eo[t, rows(slot, 0), :], rback[t, slot, 0], rback[t, slot, 1], rback[t, slot, 2]], axis=0
-        )
+    def weigh(t, weights, got):
         if t == 1:
-            return dot_rows(pick[:, :T].astype(BF), got)
+            return dot_rows((weights > 0.0).astype(F32)[:, :T].astype(BF), got)
         high = weights.astype(BF)
         low = (weights - high.astype(F32)).astype(BF)
         return dot_rows(high[:, :T], got) + dot_rows(low[:, :T], got)
+
+    def combine(t, slot):
+        weights = chooser(slot)[1]
+        if crosses(2 + t, slot):
+            got = [eo[t, rows(slot, 0), :], rback[t, slot, 0], rback[t, slot, 1], rback[t, slot, 2]]
+        else:
+            got = [eo[t, rows(slot, 0), :], rback[t, slot, 0], rback[t, slot, 2]]
+            weights = jnp.concatenate([weights[0 : 2 * C], weights[3 * C : 4 * C]], axis=0)
+        return weigh(t, weights, jnp.concatenate(got, axis=0))
+
+    d_copy, far_copy = {}, {}
+
+    def z_return(t, slot):
+        device = (z_left, z_right, z_left2, z_right2)[slot - 1]
+        d_copy[t, slot] = send(
+            eo.at[t, rows(slot, 2)], rback.at[t, slot, 1], dsend.at[t, slot], drecv.at[t, slot], device
+        )
+
+    def far_first():
+        far_copy[0] = send(far_send, far_relay, fsend.at[0], frecv.at[0], y_right)
+
+    def far_second():
+        far_copy[0].wait_recv()
+        far_copy[1] = send(far_relay, far_info, fsend.at[1], frecv.at[1], y_right)
+
+    def dense_sum(t):
+        if t not in settled:
+            settle(t)
+        if 9 not in seen:
+            seen.add(9)
+            far_copy[1].wait_recv()
+        for slot in range(1, 5):
+            d_copy[t, slot].wait_recv()
+        far = far_info[...]
+        weights = jnp.concatenate([place_rows(far[2 * i : 2 * i + 1], far[2 * i + 1 : 2 * i + 2]) for i in range(5)], axis=0)
+        got = [eo[t, rows(0, 2), :]] + [rback[t, slot, 1] for slot in range(1, 5)]
+        ag[t, 0] = weigh(t, weights, jnp.concatenate(got, axis=0)).astype(BF)
+        for i, device in ((0, y_right), (1, y_left)):
+            cols = pl.ds(i * HD, HD)
+            d_copy[t, 5 + i] = send(
+                ag.at[t, 0, :, cols], drelay.at[t, :, cols],
+                dsend.at[t, (0, 5)[i]], drecv.at[t, (0, 5)[i]], device,
+            )
+
+    def dense_relay(t):
+        for i, device in ((0, y_right), (1, y_left)):
+            cols = pl.ds(i * HD, HD)
+            d_copy[t, 5 + i].wait_recv()
+            d_copy[t, 7 + i] = send(
+                drelay.at[t, :, cols], dland.at[t, :, cols], dsend.at[t, 6 + i], drecv.at[t, 6 + i], device
+            )
+
+    settled = set()
+
+    def settle(t):
+        settled.add(t)
+        for key, copy in ag_copy.items():
+            if key[0] == t:
+                copy.wait_send()
 
     def z_step(t, slot):
         y_wait(t + 2, slot)
         total = combine(t, slot)
         if slot == 7:
-            for key, copy in ag_copy.items():
-                if key[0] == t:
-                    copy.wait_send()
+            if t not in settled:
+                settle(t)
             ag[t, 7] = total.astype(BF)
             z_copy[t, 0] = send(
                 ag.at[t, 7, :, pl.ds(0, HD)], zrecv.at[t, 0, :, pl.ds(0, HD)],
@@ -305,6 +379,9 @@
         else:
             z_copy[t, 3].wait_recv()
             z_copy[t, 7].wait_recv()
+            d_copy[t, 7].wait_recv()
+            d_copy[t, 8].wait_recv()
+            total = total + dland[t].astype(F32)
             out = layer_out if t == 0 else input_grad
             out[...] = (total + zrecv[t, 3].astype(F32) + zrecv[t, 7].astype(F32)).astype(BF)
 
@@ -331,29 +408,27 @@
         start = pl.multiple_of(((x + k) % NX * 2 + c) * 256, 256)
         parts[w][pl.ds(start, 256), :] = dot_rows(xg[0, :, pl.ds(start, 256)], grad[...]).astype(BF)
 
-    def wgrad(w, far):
+    owners = (2, 1, 3, 0)
+
+    def wgrad(w, far, part):
         if w == 0:
 
-            @pl.loop(0, D // 256)
+            @pl.loop(2 * part, 2 * part + 2)
             def _(n):
                 cols = pl.ds(pl.multiple_of(n * 256, 256), 256)
                 wd[:, cols] = dot_rows(hid[...], xg[1, :, cols]).astype(BF)
 
-            for k in (2, 1, 3, 0):
-                core_send(w, k)
+            down_parts.add(part)
+            if len(down_parts) == 4:
+                for k in owners:
+                    core_send(0, k)
         elif far:
-
-            @pl.loop(0, NX)
-            def _(k):
-                wgrad_tile(w, k, 1 - core)
-
-            for k in (2, 1, 3, 0):
-                core_send(w, k)
+            wgrad_tile(w, owners[part], 1 - core)
+            core_send(w, owners[part])
         else:
-
-            @pl.loop(0, NX)
-            def _(k):
-                wgrad_tile(w, k, core)
+            wgrad_tile(w, owners[part], core)
+
+    down_parts = set()
 
     def add_block(w, k, extra, finish=None):
         first = band_of(w, k, core)
@@ -412,25 +487,29 @@
         add_block(w, 0, (xf_of[w].at[0], xf_of[w].at[1]), outs[w])
 
     for step in (
-        (gather, 0, 1), (choose, 1, 0), (gather, 1, 1), (choose, 0, 0), (choose, 0, 2), (gather, 0, 2),
-        (choose, 0, 1), (choose, 1, 1), (gather, 1, 2), (y_relay, 0, 0), (y_relay, 0, 1), (choose, 1, 2),
-        (choose, 0, 3), (y_relay, 1, 0), (gather, 0, 3), (forward, 0), (y_relay, 0, 2), (y_relay, 1, 1),
-        (choose, 0, 4), (choose, 1, 3), (choose, 1, 4), (gather, 0, 4), (gather, 1, 3), (y_relay, 0, 3),
-        (backward, 0), (choose, 0, 5), (row_grad, 0), (choose, 0, 6), (y_relay, 1, 2), (y_relay, 0, 4),
-        (y_relay, 1, 4), (y_relay, 1, 3), (forward, 1), (down, 0), (y_relay, 0, 5), (choose, 0, 7), (gather, 1, 4),
-        (y_relay, 0, 6), (choose, 1, 5), (backward, 1), (row_grad, 1), (y_relay, 0, 7), (choose, 1, 7), (down, 1),
-        (choose, 1, 6), (y_relay, 1, 5), (forward, 2), (forward, 3), (y_relay, 1, 7), (down, 2), (y_relay, 1, 6),
-        (y_send, 2, 4), (down, 3), (y_send, 2, 7), (backward, 2), (y_send, 2, 6), (backward, 3), (y_send, 2, 5),
-        (wgrad, 1, 1), (row_grad, 3), (y_send, 3, 7), (wgrad, 1, 0), (y_send, 3, 6), (y_send, 2, 3), (y_relay, 2, 7),
-        (x_first, 1), (y_relay, 2, 6), (wgrad, 2, 1), (row_grad, 2), (y_relay, 3, 7), (wgrad, 2, 0),
-        (x_second, 1, 0), (y_send, 3, 5), (y_relay, 2, 5), (x_second, 1, 1), (y_send, 3, 4), (wgrad, 0, 1),
-        (y_send, 2, 2), (y_relay, 3, 6), (z_step, 0, 7), (y_relay, 3, 5), (y_send, 3, 3), (y_relay, 2, 3),
-        (z_step, 1, 7), (x_first, 0), (z_step, 0, 6), (z_step, 0, 5), (y_send, 2, 1), (x_first, 2), (x_last, 1),
-        (y_relay, 2, 4), (y_relay, 3, 4), (z_step, 1, 6), (z_step, 1, 5), (y_relay, 2, 2), (x_second, 0, 0),
-        (x_second, 0, 1), (y_relay, 3, 3), (y_send, 2, 0), (z_step, 0, 3), (y_send, 3, 1), (z_step, 0, 4),
-        (y_relay, 2, 1), (y_send, 3, 2), (x_second, 2, 1), (z_step, 1, 4), (z_step, 1, 3), (y_relay, 2, 0),
-        (z_step, 0, 2), (y_relay, 3, 1), (y_send, 3, 0), (y_relay, 3, 2), (x_second, 2, 0), (z_step, 0, 1),
-        (z_step, 1, 1), (y_relay, 3, 0), (x_last, 0), (z_step, 1, 2), (z_step, 0, 0), (x_last, 2), (z_step, 1, 0),
+        (gather, 0, 1), (far_first,), (gather, 1, 1), (choose, 0, 0), (choose, 1, 0), (gather, 0, 2), (choose, 0, 2),
+        (y_relay, 0, 0), (choose, 0, 1), (choose, 1, 1), (gather, 1, 2), (far_second,), (y_relay, 0, 1),
+        (choose, 1, 2), (choose, 0, 3), (gather, 0, 3), (y_relay, 1, 1), (y_relay, 1, 0), (choose, 0, 4),
+        (forward, 0), (down, 0), (y_relay, 0, 2), (y_relay, 0, 3), (gather, 1, 3), (choose, 1, 3), (backward, 0),
+        (choose, 0, 5), (choose, 0, 6), (gather, 0, 4), (y_relay, 1, 2), (y_relay, 0, 4), (gather, 1, 4),
+        (forward, 1), (y_relay, 1, 3), (choose, 0, 7), (row_grad, 0), (choose, 1, 7), (y_relay, 0, 5),
+        (choose, 1, 6), (down, 1), (y_relay, 0, 6), (backward, 1), (z_return, 0, 2), (y_relay, 0, 7), (row_grad, 1),
+        (choose, 1, 5), (y_relay, 1, 7), (choose, 1, 4), (forward, 2), (z_return, 0, 3), (y_relay, 1, 6),
+        (forward, 3), (down, 2), (z_return, 1, 2), (y_relay, 1, 5), (down, 3), (y_relay, 1, 4), (y_send, 2, 7),
+        (z_return, 1, 1), (backward, 3), (row_grad, 3), (y_send, 3, 7), (z_return, 0, 1), (backward, 2),
+        (z_return, 1, 3), (wgrad, 2, 1, 0), (wgrad, 1, 1, 0), (wgrad, 2, 0, 0), (y_relay, 2, 7), (y_send, 3, 6),
+        (row_grad, 2), (y_send, 2, 6), (y_relay, 3, 7), (y_send, 3, 5), (wgrad, 2, 0, 1), (x_first, 2),
+        (y_send, 2, 5), (wgrad, 2, 1, 2), (z_return, 0, 4), (wgrad, 2, 0, 2), (wgrad, 1, 0, 0), (z_step, 0, 7),
+        (wgrad, 2, 1, 1), (x_first, 1), (wgrad, 0, 1, 1), (wgrad, 0, 1, 0), (wgrad, 1, 1, 1), (y_relay, 3, 5),
+        (z_step, 1, 7), (y_relay, 3, 6), (y_relay, 2, 6), (x_second, 2, 0), (x_second, 2, 1), (y_send, 3, 3),
+        (z_return, 1, 4), (wgrad, 0, 1, 2), (y_relay, 2, 5), (wgrad, 1, 1, 2), (z_step, 1, 5), (y_send, 3, 1),
+        (y_send, 3, 4), (y_send, 2, 2), (z_step, 1, 6), (wgrad, 0, 1, 3), (z_step, 0, 6), (y_send, 2, 4),
+        (y_send, 2, 3), (z_step, 0, 5), (x_first, 0), (y_send, 3, 2), (wgrad, 1, 0, 2), (wgrad, 1, 0, 1),
+        (y_send, 3, 0), (x_second, 1, 0), (z_step, 1, 3), (z_step, 1, 4), (x_second, 1, 1), (y_send, 2, 1),
+        (z_step, 0, 4), (dense_sum, 1), (z_step, 0, 3), (x_second, 0, 0), (y_send, 2, 0), (z_step, 1, 2),
+        (x_second, 0, 1), (wgrad, 2, 1, 3), (z_step, 1, 1), (dense_sum, 0), (z_step, 0, 2), (dense_relay, 1),
+        (z_step, 0, 1), (wgrad, 1, 1, 3), (dense_relay, 0), (wgrad, 2, 0, 3), (wgrad, 1, 0, 3), (z_step, 1, 0),
+        (x_last, 2), (x_last, 1), (z_step, 0, 0), (x_last, 0),
     ):
         step[0](*step[1:])
 
@@ -467,6 +546,12 @@
         scratch_shapes=[
             V((8, T), jnp.int32),
             V((8, T), F32),
+            V((NZ, NY * C, 128), F32),
+            V((16, 128), F32),
+            V((16, 128), F32),
+            V((16, 128), F32),
+            V((2, T, D), BF),
+            V((2, T, D), BF),
             V((2, NZ, T, D), BF),
             V((NZ, NZ, 8, 128), F32),
             V((2, NZ, 3, C, D), BF),
@@ -504,6 +589,10 @@
             dma((3, NX)),
             dma((3, 4)),
             dma((3, 4)),
+            dma((2,)),
+            dma((2,)),
+            dma((2, 8)),
+            dma((2, 8)),
         ],
         compiler_params=pltpu.CompilerParams(
             collective_id=0, has_side_effects=True, vmem_limit_bytes=63_900_000

time: 119 us -> 116 us (0.975)
  Pallas kernels: 117 us -> 113 us
    pallas_call x1, Pallas kernels: 115 us -> 112 us  [shards(): pl.pallas_call(kernel, out_shape=(V((T, D), BF), V((T, D), BF), V((D // 8...]
where the time goes in v3:
time: 116 us; the launch traced here: 114 us
  Pallas kernels  113 us (97%)
    pallas_call x1, Pallas kernels, shards(): pl.pallas_call(kernel, out_shape=(V((T, D), BF), V((T, D), BF), V((D // 8...  112 us

profile of v3, /device:TPU:8, one launch (start us, length us, event | category | flops | bytes accessed | tf_op | source)
XLA Modules:
  0.0 114.3 jit_solution(4491155605357590263)
XLA Ops:
  0.6 111.9 %expert_layer.1 = (bf16[48,2048]{1,0:T(8,128)(2,1)S(1)}, bf16[48,2048]{1,0:T(8,128)(2,1)S(1)}, f32[256,768]{1,0:T(8,128)S(1)}, f32[256,768]{1,0:T(8,128)S(1)}, f32[96,2048]{1,0:T(8,128)S(1)}) custom-call(s32[8,48]{1,0:T(8,128)} %bitcast.11, f32[8,48]{1,0:T(8,128)} %bitcast.12, bf16[48,2048]{1,0:T(8,128)(2,1)} %tok_hbm.1, bf16[48,2048]{1,0:T(8,128)(2,1)} %cot_hbm.1, ...), custom_call_target="tpu_custom_call" | custom-call | tf_op jit(solution)/shard_map/expert_layer/pallas_call | solution.py:535
  112.5 1.6 %store.1 = (bf16[48,2048]{1,0:T(8,128)(2,1)}, bf16[48,2048]{1,0:T(8,128)(2,1)}, f32[256,768]{1,0:T(8,128)}, f32[256,768]{1,0:T(8,128)}, f32[96,2048]{1,0:T(8,128)}) custom-call(bf16[48,2048]{1,0:T(8,128)(2,1)S(1)} %get-tuple-element.15.refs_0_, bf16[48,2048]{1,0:T(8,128)(2,1)S(1)} %get-tuple-element.16.refs_1_, f32[256,768]{1,0:T(8,128)S(1)} %get-tuple-element.17.refs_2_, ...), custom_call_target="tpu_custom_call" | custom-call | tf_op jit(solution)/shard_map/store/pallas_call | solution.py:602

commit v4 on v3

--- a/solution.py
+++ b/solution.py
@@ -31,10 +31,10 @@
 def kernel(
     ids_hbm, probs_hbm, tok_hbm, cot_hbm, wg_hbm, wu_hbm, wd_hbm,
     layer_out, input_grad, gate_out, up_out, down_out,
-    ids, probs, chooser_rows, far_send, far_relay, far_info, drelay, dland, ag, ai, sb, xg, eo, rback, relay, wg, wu, wd, gp, up, hid, gg, ug,
+    ids, probs, chooser_rows, far_send, far_relay, far_info, far_rows, prelay, pland, drelay, dland, ag, ai, sb, xg, eo, rback, relay, wg, wu, wd, gp, up, hid, gg, ug,
     zrecv, pg, pu, cr_a, cr_d, xh_a, xh_d, xf_a, xf_d,
     loc, ysend, yrecv, asend, arecv, isend, irecv, zsend, zrecv_sem, csend, crecv, xsend, xrecv, fsend, frecv,
-    dsend, drecv,
+    dsend, drecv, psend, precv,
 ):
     ex = lax.axis_index("expert")
     dp = lax.axis_index("dp")
@@ -108,6 +108,12 @@
 
     loaded = set()
 
+    def own_block(t):
+        if t not in loaded:
+            loads[2 + t].wait()
+            loaded.add(t)
+
+
     ag_copy = {}
 
     def ag_step(t, step):
@@ -145,9 +151,7 @@
 
     def gather(t, step):
         if step == 1:
-            if t not in loaded:
-                loads[2 + t].wait()
-                loaded.add(t)
+            own_block(t)
         else:
             ag_wait(t, (2 * step - 3, 2 * step - 2))
         ag_step(t, step)
@@ -166,7 +170,9 @@
                 yy = (y + r) % NY
                 chooser_rows[slot, r * C : (r + 1) * C, :] = place_rows(line_of(table, yy), line_of(table, yy + 4))
         weights = chooser_rows[slot]
-        return (weights > 0.0).astype(F32), weights
+        if slot >= 5:
+            return weights, (0, 1, 2, 3)
+        return jnp.concatenate([weights[0 : 2 * C], weights[3 * C : 4 * C]], axis=0), (0, 1, 3)
 
     y_copy = {}
 
@@ -179,11 +185,8 @@
     def y_src(t, slot, r):
         return sb.at[t, slot, r - 1] if t < 2 else eo.at[t - 2, rows(slot, r)]
 
-    def crosses(t, slot):
-        return t < 2 or slot >= 5
-
     def relay_side(t, slot):
-        return y_right if (slot + (t if slot == 7 and t >= 2 else 0)) % 2 == 0 else y_left
+        return y_right if (slot + (t if slot == 7 else 0)) % 2 == 0 else y_left
 
     def y_send(t, slot):
         y_copy[t, slot, 0] = send(
@@ -192,46 +195,53 @@
         y_copy[t, slot, 1] = send(
             y_src(t, slot, 3), y_dst(t, slot, 1), ysend.at[t, slot, 1], yrecv.at[t, slot, 1], y_left
         )
-        if crosses(t, slot):
+        if slot >= 5:
             y_copy[t, slot, 2] = send(
-                y_src(t, slot, 2), relay.at[t, slot], ysend.at[t, slot, 2], yrecv.at[t, slot, 2], relay_side(t, slot)
+                y_src(t, slot, 2), relay.at[t, slot - 5], ysend.at[t, slot, 2], yrecv.at[t, slot, 2], relay_side(t, slot)
             )
 
     def y_relay(t, slot):
         y_copy[t, slot, 2].wait_recv()
         y_copy[t, slot, 3] = send(
-            relay.at[t, slot], y_dst(t, slot, 2), ysend.at[t, slot, 3], yrecv.at[t, slot, 3], relay_side(t, slot)
+            relay.at[t, slot - 5], y_dst(t, slot, 2), ysend.at[t, slot, 3], yrecv.at[t, slot, 3], relay_side(t, slot)
         )
 
     def y_wait(t, *slots):
         for slot in slots:
             for i in (0, 1, 3):
-                if i < 3 or crosses(t, slot):
+                if i < 3 or slot >= 5:
                     y_copy[t, slot, i].wait_recv()
+            if t < 2 and 1 <= slot <= 4:
+                p_copy[t, slot].wait_recv()
+
+    def pick_rows(t, weights, block):
+        chosen = dot((weights > 0.0).astype(F32)[:, :T].astype(BF), block)
+        if t == 1:
+            chosen = chosen * jnp.sum(weights, axis=1, keepdims=True)
+        return chosen.astype(BF)
 
     def choose(t, slot):
         if slot > 0:
             ag_wait(t, (slot,))
-        elif t not in loaded:
-            loads[2 + t].wait()
-            loaded.add(t)
-        pick, weights = chooser(slot)
-        chosen = dot(pick[:, :T].astype(BF), ag[t, slot])
-        if t == 1:
-            chosen = chosen * jnp.sum(weights, axis=1, keepdims=True)
-        chosen = chosen.astype(BF)
-        xg[t, rows(slot, 0), :] = chosen[0:C, :]
-        for r in range(1, NY):
-            sb[t, slot, r - 1] = chosen[r * C : (r + 1) * C, :]
+        else:
+            own_block(t)
+        weights, groups = chooser(slot)
+        chosen = pick_rows(t, weights, ag[t, slot])
+        for i, r in enumerate(groups):
+            if r == 0:
+                xg[t, rows(slot, 0), :] = chosen[0:C, :]
+            else:
+                sb[t, slot, r - 1] = chosen[i * C : (i + 1) * C, :]
         y_send(t, slot)
 
-    down_ready = []
+    down_ready, up_ready = [], []
 
     def forward(c):
         y_wait(0, 2 * c, 2 * c + 1)
-        if c == 0:
+        if not up_ready:
             loads[4].wait()
             loads[5].wait()
+            up_ready.append(c)
         band = pl.ds(c * 128, 128)
 
         @pl.loop(0, F // 256)
@@ -288,12 +298,8 @@
         return dot_rows(high[:, :T], got) + dot_rows(low[:, :T], got)
 
     def combine(t, slot):
-        weights = chooser(slot)[1]
-        if crosses(2 + t, slot):
-            got = [eo[t, rows(slot, 0), :], rback[t, slot, 0], rback[t, slot, 1], rback[t, slot, 2]]
-        else:
-            got = [eo[t, rows(slot, 0), :], rback[t, slot, 0], rback[t, slot, 2]]
-            weights = jnp.concatenate([weights[0 : 2 * C], weights[3 * C : 4 * C]], axis=0)
+        weights, groups = chooser(slot)
+        got = [eo[t, rows(slot, 0), :]] + [rback[t, slot, r - 1] for r in groups[1:]]
         return weigh(t, weights, jnp.concatenate(got, axis=0))
 
     d_copy, far_copy = {}, {}
@@ -311,16 +317,56 @@
         far_copy[0].wait_recv()
         far_copy[1] = send(far_relay, far_info, fsend.at[1], frecv.at[1], y_right)
 
+    p_copy = {}
+
+    def dense_first(t):
+        own_block(t)
+        if t == 0:
+            far_first()
+        for i, device in ((0, y_right), (1, y_left)):
+            cols = pl.ds(i * HD, HD)
+            p_copy[t, 5 + i] = send(
+                ag.at[t, 0, :, cols], prelay.at[t, :, cols],
+                psend.at[t, (0, 5)[i]], precv.at[t, (0, 5)[i]], device,
+            )
+
+    def dense_pass(t):
+        if t == 0:
+            far_second()
+        for i, device in ((0, y_right), (1, y_left)):
+            cols = pl.ds(i * HD, HD)
+            p_copy[t, 5 + i].wait_recv()
+            p_copy[t, 7 + i] = send(
+                prelay.at[t, :, cols], pland.at[t, :, cols], psend.at[t, 6 + i], precv.at[t, 6 + i], device
+            )
+
+    def far_ready():
+        if 9 not in seen:
+            seen.add(9)
+            far_copy[1].wait_recv()
+            far = far_info[...]
+            for i in range(5):
+                far_rows[i * C : (i + 1) * C, :] = place_rows(far[2 * i : 2 * i + 1], far[2 * i + 1 : 2 * i + 2])
+        return far_rows[...]
+
+    def dense_choose(t):
+        p_copy[t, 7].wait_recv()
+        p_copy[t, 8].wait_recv()
+        chosen = pick_rows(t, far_ready(), pland[t])
+        xg[t, rows(0, 2), :] = chosen[0:C, :]
+        for slot in (3, 4, 1, 2):
+            sb[t, slot, 1] = chosen[slot * C : (slot + 1) * C, :]
+            device = (z_right, z_left, z_right2, z_left2)[slot - 1]
+            p_copy[t, slot] = send(
+                sb.at[t, slot, 1], xg.at[t, rows(slot, 2)], psend.at[t, slot], precv.at[t, slot], device
+            )
+
     def dense_sum(t):
         if t not in settled:
             settle(t)
-        if 9 not in seen:
-            seen.add(9)
-            far_copy[1].wait_recv()
+        weights = far_ready()
         for slot in range(1, 5):
             d_copy[t, slot].wait_recv()
-        far = far_info[...]
-        weights = jnp.concatenate([place_rows(far[2 * i : 2 * i + 1], far[2 * i + 1 : 2 * i + 2]) for i in range(5)], axis=0)
         got = [eo[t, rows(0, 2), :]] + [rback[t, slot, 1] for slot in range(1, 5)]
         ag[t, 0] = weigh(t, weights, jnp.concatenate(got, axis=0)).astype(BF)
         for i, device in ((0, y_right), (1, y_left)):
@@ -338,13 +384,17 @@
                 drelay.at[t, :, cols], dland.at[t, :, cols], dsend.at[t, 6 + i], drecv.at[t, 6 + i], device
             )
 
-    settled = set()
+    settled, finished = set(), []
 
     def settle(t):
         settled.add(t)
         for key, copy in ag_copy.items():
             if key[0] == t:
                 copy.wait_send()
+                finished.append(id(copy))
+        for k in (5, 6):
+            p_copy[t, k].wait_send()
+            finished.append(id(p_copy[t, k]))
 
     def z_step(t, slot):
         y_wait(t + 2, slot)
@@ -487,35 +537,33 @@
         add_block(w, 0, (xf_of[w].at[0], xf_of[w].at[1]), outs[w])
 
     for step in (
-        (gather, 0, 1), (far_first,), (gather, 1, 1), (choose, 0, 0), (choose, 1, 0), (gather, 0, 2), (choose, 0, 2),
-        (y_relay, 0, 0), (choose, 0, 1), (choose, 1, 1), (gather, 1, 2), (far_second,), (y_relay, 0, 1),
-        (choose, 1, 2), (choose, 0, 3), (gather, 0, 3), (y_relay, 1, 1), (y_relay, 1, 0), (choose, 0, 4),
-        (forward, 0), (down, 0), (y_relay, 0, 2), (y_relay, 0, 3), (gather, 1, 3), (choose, 1, 3), (backward, 0),
-        (choose, 0, 5), (choose, 0, 6), (gather, 0, 4), (y_relay, 1, 2), (y_relay, 0, 4), (gather, 1, 4),
-        (forward, 1), (y_relay, 1, 3), (choose, 0, 7), (row_grad, 0), (choose, 1, 7), (y_relay, 0, 5),
-        (choose, 1, 6), (down, 1), (y_relay, 0, 6), (backward, 1), (z_return, 0, 2), (y_relay, 0, 7), (row_grad, 1),
-        (choose, 1, 5), (y_relay, 1, 7), (choose, 1, 4), (forward, 2), (z_return, 0, 3), (y_relay, 1, 6),
-        (forward, 3), (down, 2), (z_return, 1, 2), (y_relay, 1, 5), (down, 3), (y_relay, 1, 4), (y_send, 2, 7),
-        (z_return, 1, 1), (backward, 3), (row_grad, 3), (y_send, 3, 7), (z_return, 0, 1), (backward, 2),
-        (z_return, 1, 3), (wgrad, 2, 1, 0), (wgrad, 1, 1, 0), (wgrad, 2, 0, 0), (y_relay, 2, 7), (y_send, 3, 6),
-        (row_grad, 2), (y_send, 2, 6), (y_relay, 3, 7), (y_send, 3, 5), (wgrad, 2, 0, 1), (x_first, 2),
-        (y_send, 2, 5), (wgrad, 2, 1, 2), (z_return, 0, 4), (wgrad, 2, 0, 2), (wgrad, 1, 0, 0), (z_step, 0, 7),
-        (wgrad, 2, 1, 1), (x_first, 1), (wgrad, 0, 1, 1), (wgrad, 0, 1, 0), (wgrad, 1, 1, 1), (y_relay, 3, 5),
-        (z_step, 1, 7), (y_relay, 3, 6), (y_relay, 2, 6), (x_second, 2, 0), (x_second, 2, 1), (y_send, 3, 3),
-        (z_return, 1, 4), (wgrad, 0, 1, 2), (y_relay, 2, 5), (wgrad, 1, 1, 2), (z_step, 1, 5), (y_send, 3, 1),
-        (y_send, 3, 4), (y_send, 2, 2), (z_step, 1, 6), (wgrad, 0, 1, 3), (z_step, 0, 6), (y_send, 2, 4),
-        (y_send, 2, 3), (z_step, 0, 5), (x_first, 0), (y_send, 3, 2), (wgrad, 1, 0, 2), (wgrad, 1, 0, 1),
-        (y_send, 3, 0), (x_second, 1, 0), (z_step, 1, 3), (z_step, 1, 4), (x_second, 1, 1), (y_send, 2, 1),
-        (z_step, 0, 4), (dense_sum, 1), (z_step, 0, 3), (x_second, 0, 0), (y_send, 2, 0), (z_step, 1, 2),
-        (x_second, 0, 1), (wgrad, 2, 1, 3), (z_step, 1, 1), (dense_sum, 0), (z_step, 0, 2), (dense_relay, 1),
-        (z_step, 0, 1), (wgrad, 1, 1, 3), (dense_relay, 0), (wgrad, 2, 0, 3), (wgrad, 1, 0, 3), (z_step, 1, 0),
-        (x_last, 2), (x_last, 1), (z_step, 0, 0), (x_last, 0),
+        (dense_first, 1), (gather, 0, 1), (dense_first, 0), (gather, 1, 1), (gather, 0, 2), (dense_pass, 1),
+        (dense_pass, 0), (choose, 1, 2), (gather, 1, 2), (choose, 1, 1), (choose, 1, 0), (choose, 0, 0),
+        (choose, 0, 4), (gather, 0, 3), (choose, 0, 1), (choose, 0, 2), (choose, 1, 4), (choose, 0, 3),
+        (gather, 1, 3), (dense_choose, 0), (choose, 1, 3), (choose, 0, 6), (gather, 0, 4), (choose, 0, 5),
+        (choose, 1, 5), (gather, 1, 4), (choose, 1, 6), (dense_choose, 1), (y_relay, 0, 5), (y_relay, 0, 6),
+        (forward, 1), (y_relay, 1, 5), (forward, 0), (y_relay, 1, 6), (choose, 0, 7), (down, 1), (down, 0),
+        (choose, 1, 7), (forward, 2), (down, 2), (z_return, 0, 2), (y_relay, 0, 7), (y_send, 2, 5), (backward, 2),
+        (backward, 1), (y_relay, 1, 7), (backward, 0), (forward, 3), (down, 3), (y_send, 2, 7), (y_send, 2, 6),
+        (z_return, 0, 3), (backward, 3), (wgrad, 2, 1, 0), (wgrad, 2, 0, 0), (row_grad, 3), (z_return, 0, 1),
+        (z_return, 0, 4), (y_send, 3, 7), (row_grad, 2), (x_first, 2), (y_relay, 2, 7), (wgrad, 1, 1, 0),
+        (wgrad, 2, 1, 1), (z_return, 1, 4), (y_send, 3, 6), (wgrad, 1, 0, 0), (wgrad, 2, 1, 2), (y_relay, 2, 5),
+        (wgrad, 0, 1, 1), (row_grad, 1), (x_first, 1), (y_relay, 3, 7), (z_return, 1, 3), (y_send, 3, 5),
+        (wgrad, 0, 1, 0), (z_step, 0, 7), (y_relay, 2, 6), (wgrad, 2, 0, 2), (wgrad, 2, 0, 1), (z_return, 1, 2),
+        (y_relay, 3, 6), (x_second, 2, 0), (y_send, 2, 0), (x_second, 2, 1), (z_step, 1, 7), (wgrad, 1, 1, 2),
+        (y_relay, 3, 5), (y_send, 3, 3), (wgrad, 1, 1, 1), (y_send, 2, 3), (z_step, 0, 5), (z_step, 0, 6),
+        (wgrad, 0, 1, 2), (wgrad, 0, 1, 3), (wgrad, 1, 0, 1), (y_send, 3, 4), (z_step, 1, 5), (y_send, 2, 4),
+        (wgrad, 1, 0, 2), (z_step, 1, 6), (y_send, 2, 1), (x_first, 0), (z_step, 0, 3), (x_second, 1, 0),
+        (x_second, 1, 1), (y_send, 3, 2), (z_step, 0, 4), (row_grad, 0), (z_return, 1, 1), (y_send, 2, 2),
+        (z_step, 1, 3), (z_step, 1, 4), (x_second, 0, 1), (y_send, 3, 1), (y_send, 3, 0), (dense_sum, 0),
+        (z_step, 0, 2), (x_second, 0, 0), (z_step, 0, 1), (dense_sum, 1), (z_step, 1, 1), (wgrad, 2, 1, 3),
+        (dense_relay, 0), (z_step, 1, 2), (wgrad, 1, 1, 3), (dense_relay, 1), (wgrad, 2, 0, 3), (z_step, 0, 0),
+        (wgrad, 1, 0, 3), (x_last, 1), (x_last, 2), (z_step, 1, 0), (x_last, 0),
     ):
         step[0](*step[1:])
 
-    early = [id(copy) for key, copy in ag_copy.items() if key[0] < 2]
     for copy in started:
-        if id(copy) not in early:
+        if id(copy) not in finished:
             copy.wait_send()
 
 
@@ -550,6 +598,9 @@
             V((16, 128), F32),
             V((16, 128), F32),
             V((16, 128), F32),
+            V((5 * C, 128), F32),
+            V((2, T, D), BF),
+            V((2, T, D), BF),
             V((2, T, D), BF),
             V((2, T, D), BF),
             V((2, NZ, T, D), BF),
@@ -558,7 +609,7 @@
             V((2, ROWS, D), BF),
             V((2, ROWS, D), BF),
             V((2, NZ, 3, C, D), BF),
-            V((4, NZ, C, D), BF),
+            V((4, 3, C, D), BF),
             V((D, F), BF),
             V((D, F), BF),
             V((F, D), BF),
@@ -593,6 +644,8 @@
             dma((2,)),
             dma((2, 8)),
             dma((2, 8)),
+            dma((2, 8)),
+            dma((2, 8)),
         ],
         compiler_params=pltpu.CompilerParams(
             collective_id=0, has_side_effects=True, vmem_limit_bytes=63_900_000

time: 116 us -> 118 us (1.017)
  Pallas kernels: 113 us -> 116 us
    pallas_call x1, Pallas kernels: 112 us -> 114 us  [shards(): pl.pallas_call(kernel, out_shape=(V((T, D), BF), V((T, D), BF), V((D // 8...]
where the time goes in v4:
time: 118 us; the launch traced here: 116 us
  Pallas kernels  116 us (98%)
    pallas_call x1, Pallas kernels, shards(): pl.pallas_call(kernel, out_shape=(V((T, D), BF), V((T, D), BF), V((D // 8...  114 us

profile of v4, /device:TPU:8, one launch (start us, length us, event | category | flops | bytes accessed | tf_op | source)
XLA Modules:
  0.0 116.4 jit_solution(7909638674336337205)
XLA Ops:
  0.6 114.1 %expert_layer.1 = (bf16[48,2048]{1,0:T(8,128)(2,1)S(1)}, bf16[48,2048]{1,0:T(8,128)(2,1)S(1)}, f32[256,768]{1,0:T(8,128)S(1)}, f32[256,768]{1,0:T(8,128)S(1)}, f32[96,2048]{1,0:T(8,128)S(1)}) custom-call(s32[8,48]{1,0:T(8,128)} %bitcast.11, f32[8,48]{1,0:T(8,128)} %bitcast.12, bf16[48,2048]{1,0:T(8,128)(2,1)} %tok_hbm.1, bf16[48,2048]{1,0:T(8,128)(2,1)} %cot_hbm.1, ...), custom_call_target="tpu_custom_call" | custom-call | tf_op jit(solution)/shard_map/expert_layer/pallas_call | solution.py:583
  114.7 1.6 %store.1 = (bf16[48,2048]{1,0:T(8,128)(2,1)}, bf16[48,2048]{1,0:T(8,128)(2,1)}, f32[256,768]{1,0:T(8,128)}, f32[256,768]{1,0:T(8,128)}, f32[96,2048]{1,0:T(8,128)}) custom-call(bf16[48,2048]{1,0:T(8,128)(2,1)S(1)} %get-tuple-element.15.refs_0_, bf16[48,2048]{1,0:T(8,128)(2,1)S(1)} %get-tuple-element.16.refs_1_, f32[256,768]{1,0:T(8,128)S(1)} %get-tuple-element.17.refs_2_, ...), custom_call_target="tpu_custom_call" | custom-call | tf_op jit(solution)/shard_map/store/pallas_call | solution.py:655
